TPU v7x, 32 devices: a whole 2x2x4 slice. The times are simulated.
32 devices in a mesh: pb: 8 (over z, x), ka: 4 (over y, core).
Axes of the slice: x: 2, y: 2, z: 4, core: 2. Of those that a mesh axis runs over, the one named last changes fastest.
Arguments:
- node_states: float32 [512, 256], P('pb'), may hold values from -17 to 17
- frames: float32 [12, 512], P(None, 'pb'), may hold values from -20 to 20, as said below
- edge_states: bfloat16 [512, 512, 128], P('pb', 'ka'), may hold values from -6 to 6
- chain_number: int32 [512], replicated, may hold values from 0 to 3, as said below
- residue_index: int32 [512], replicated, may hold values from 0 to 767, as said below
- padding_mask: int32 [512], replicated, may hold values from 0 to 1, as said below
- query_weight: bfloat16 [256, 2048], replicated, may hold values from -0.375 to 0.375
- key_weight: bfloat16 [256, 2048], replicated, may hold values from -0.375 to 0.375
- value_weight: bfloat16 [256, 2048], replicated, may hold values from -0.375 to 0.375
- point_query: bfloat16 [256, 192], replicated, may hold values from -0.375 to 0.375
- point_key: bfloat16 [256, 192], replicated, may hold values from -0.375 to 0.375
- point_value: bfloat16 [256, 288], replicated, may hold values from -0.375 to 0.375
- bias_weight: bfloat16 [128, 8], replicated, may hold values from -0.5 to 0.5
- point_gamma: float32 [8], replicated, may hold values from 0.3 to 3
- relpos_table: float32 [128, 128], replicated, may hold values from -3 to 3
- output_weight: bfloat16 [3456, 256], replicated, may hold values from -0.109375 to 0.109375
- attention_scales: float32 [256], replicated, may hold values from 0.5 to 1.5
- layer_project: bfloat16 [2, 256, 768], replicated, may hold values from -0.375 to 0.375
- layer_output: bfloat16 [2, 256, 256], replicated, may hold values from -0.375 to 0.375
- layer_expand: bfloat16 [2, 256, 256], replicated, may hold values from -0.375 to 0.375
- layer_shrink: bfloat16 [2, 256, 256], replicated, may hold values from -0.375 to 0.375
- layer_scales: float32 [2, 2, 256], replicated, may hold values from 0.5 to 1.5
- frame_weight: float32 [256, 6], replicated, may hold values from -0.375 to 0.375
- node_to_edge: bfloat16 [256, 768], replicated, may hold values from -0.375 to 0.375
- edge_first: bfloat16 [128, 384], replicated, may hold values from -0.5 to 0.5
- edge_second: bfloat16 [384, 384], replicated, may hold values from -0.3125 to 0.3125
- edge_third: bfloat16 [384, 128], replicated, may hold values from -0.3125 to 0.3125
- edge_biases: float32 [2, 384], replicated, may hold values from -3 to 3
- edge_scales: float32 [128], replicated, may hold values from 0.5 to 1.5
Outputs:
- node_out: float32 [512, 256], P('pb')
- frames_out: float32 [12, 512], P(None, 'pb')
- edges_out: bfloat16 [512, 512, 128], P('pb', 'ka')
Inputs may be any that keep to these rules, and one draw needn't show every extreme that they name: `chain_number`: never falls from one residue to the next; the first residue has 0 and the last 3. `residue_index`: rises by 1 or 2 from one residue to the next, starting at 0; exactly 256 of the rises are 2. `padding_mask`: the ones come first; at least 256 residues are ones and at least one is padding. `frames`: rows 0 to 8 form a proper rotation of each residue.
All inputs are finite; a program needn't handle non-finite values.
Results may differ from a plain program's by a relative error of at most 0.025.
Values may be sent and summed in bfloat16 or wider, within the bound.
A program may use at most 128 MiB of HBM per device.

v0:
```python
import functools
import math

import jax
import jax.numpy as jnp
from jax import lax
from jax.experimental import pallas as pl
from jax.experimental.pallas import tpu as pltpu
from jax.sharding import PartitionSpec as P

C_S = 256
HEADS = 8
HD = 256
QKP = 8
VP = 12
EH = 384
RELBINS = 128
LAYERS = 2
TF_HD = 64


HIGHEST = lax.Precision.HIGHEST
NEG_FILL = -1000000000.0


def layer_norm(values, scales):
    centered = values - jnp.mean(values, axis=-1, keepdims=True)
    variance = jnp.mean(centered * centered, axis=-1, keepdims=True)
    return centered * lax.rsqrt(variance + 1e-05) * scales


def frame_parts(frames):
    rotation = jnp.transpose(frames[:9]).reshape(-1, 3, 3)
    offset = jnp.transpose(frames[9:12])
    return (rotation, offset)


def head_split(matrix, width):
    return matrix.reshape(matrix.shape[0], -1, width)


def place_points(features, weight, rotation, offset, count):
    local = jnp.dot(features, weight, preferred_element_type=jnp.float32)
    local = local.reshape(local.shape[0], HEADS, 3, count)
    placed = jnp.einsum("rcd,rhdp->rhcp", rotation, local, precision=HIGHEST)
    return placed + offset[:, None, :, None]


def relative_bins(chain_rows, index_rows, chain_cols, index_cols):
    reach = (RELBINS - 2) // 2
    gap_class = jnp.clip(index_rows[:, None] - index_cols[None, :], -reach, reach) + reach
    same_chain = chain_rows[:, None] == chain_cols[None, :]
    return jnp.where(same_chain, gap_class, RELBINS - 1)


def point_logits(
    queries, key_vectors, query_places, key_places, pair_rep, bias_weight, point_gamma
):
    scalar = jnp.einsum(
        "ihd,jhd->hij", queries, key_vectors, preferred_element_type=jnp.float32
    ) / math.sqrt(HD)
    pair_bias = jnp.einsum("ijc,ch->hij", pair_rep, bias_weight, preferred_element_type=jnp.float32)
    query_square = jnp.sum(query_places * query_places, axis=(2, 3))
    key_square = jnp.sum(key_places * key_places, axis=(2, 3))
    cross = jnp.einsum("ihcp,jhcp->hij", query_places, key_places, precision=HIGHEST)
    distance = (
        jnp.transpose(query_square)[:, :, None]
        + jnp.transpose(key_square)[:, None, :]
        - 2.0 * cross
    )
    weight_points = math.sqrt(2.0 / (9.0 * QKP))
    return math.sqrt(1.0 / 3.0) * (
        scalar + pair_bias - 0.5 * weight_points * point_gamma[:, None, None] * distance
    )


def ipa_features(scalar_out, pair_out, point_global, rotation, offset):
    moved = point_global - offset[:, None, :, None]
    local = jnp.einsum("icd,ihcp->ihdp", rotation, moved, precision=HIGHEST)
    lengths = jnp.sqrt(jnp.sum(local * local, axis=2) + 1e-08)
    count = scalar_out.shape[0]
    return jnp.concatenate(
        [
            scalar_out.reshape(count, -1),
            pair_out.reshape(count, -1),
            local.reshape(count, -1),
            lengths.reshape(count, -1),
        ],
        axis=1,
    )


def encoder_core(states, query_half, key_value, valid, output, expand, shrink, scales):
    queries = head_split(query_half, TF_HD)
    key_vectors = head_split(key_value[:, :C_S], TF_HD)
    value_vectors = head_split(key_value[:, C_S:], TF_HD)
    scores = jnp.einsum(
        "ihd,jhd->hij", queries, key_vectors, preferred_element_type=jnp.float32
    ) / math.sqrt(TF_HD)
    masked = jnp.where(valid[None, None, :], scores, NEG_FILL)
    row_top = jnp.max(masked, axis=-1, keepdims=True)
    weights = jnp.where(valid[None, None, :], jnp.exp(masked - row_top), 0.0)
    attention = (weights / jnp.sum(weights, axis=-1, keepdims=True)).astype(jnp.bfloat16)
    context = jnp.einsum(
        "hij,jhd->ihd", attention, value_vectors, preferred_element_type=jnp.float32
    ).astype(jnp.bfloat16)
    context = context.reshape(states.shape[0], C_S)
    middle = layer_norm(
        states + jnp.dot(context, output, preferred_element_type=jnp.float32), scales[0]
    )
    hidden = jax.nn.relu(
        jnp.dot(middle.astype(jnp.bfloat16), expand, preferred_element_type=jnp.float32)
    ).astype(jnp.bfloat16)
    return layer_norm(
        middle + jnp.dot(hidden, shrink, preferred_element_type=jnp.float32), scales[1]
    )


def update_frames(states, frames, frame_weight):
    update = jnp.dot(states, frame_weight, precision=HIGHEST)
    length = jnp.sqrt(
        1.0
        + update[:, 0] * update[:, 0]
        + update[:, 1] * update[:, 1]
        + update[:, 2] * update[:, 2]
    )
    real_part = 1.0 / length
    first_imag = update[:, 0] / length
    second_imag = update[:, 1] / length
    third_imag = update[:, 2] / length
    row_one = jnp.stack(
        [
            real_part * real_part
            + first_imag * first_imag
            - second_imag * second_imag
            - third_imag * third_imag,
            2.0 * (first_imag * second_imag - real_part * third_imag),
            2.0 * (first_imag * third_imag + real_part * second_imag),
        ],
        axis=1,
    )
    row_two = jnp.stack(
        [
            2.0 * (first_imag * second_imag + real_part * third_imag),
            real_part * real_part
            - first_imag * first_imag
            + second_imag * second_imag
            - third_imag * third_imag,
            2.0 * (second_imag * third_imag - real_part * first_imag),
        ],
        axis=1,
    )
    row_three = jnp.stack(
        [
            2.0 * (first_imag * third_imag - real_part * second_imag),
            2.0 * (second_imag * third_imag + real_part * first_imag),
            real_part * real_part
            - first_imag * first_imag
            - second_imag * second_imag
            + third_imag * third_imag,
        ],
        axis=1,
    )
    turn = jnp.stack([row_one, row_two, row_three], axis=1)
    rotation, offset = frame_parts(frames)
    new_rotation = jnp.einsum("rcd,rde->rce", rotation, turn, precision=HIGHEST)
    new_offset = jnp.einsum("rcd,rd->rc", rotation, update[:, 3:6], precision=HIGHEST) + offset
    return jnp.transpose(jnp.concatenate([new_rotation.reshape(-1, 9), new_offset], axis=1))


MESH = pl.DeviceIdType.MESH


def greet(peers):
    barrier = pltpu.get_barrier_semaphore()
    for peer in peers:
        pl.semaphore_signal(barrier, inc=1, device_id=peer, device_id_type=MESH)
    pl.semaphore_wait(barrier, len(peers))


def key_tile_kernel(n_pb, n_ka, x_ref, o_ref, send, recv, own):
    row, col = lax.axis_index("pb"), lax.axis_index("ka")
    per = n_pb // n_ka
    peers = [{"pb": lax.rem(row + d, n_pb)} for d in range(1, n_pb)]
    greet(peers)
    for slot in range(per):

        @pl.when(row == col * per + slot)
        def _():
            local = pltpu.make_async_copy(x_ref, o_ref.at[slot], own)
            local.start()
            copies = [
                pltpu.make_async_remote_copy(
                    src_ref=x_ref,
                    dst_ref=o_ref.at[slot],
                    send_sem=send.at[d],
                    recv_sem=recv.at[slot],
                    device_id=peer,
                    device_id_type=MESH,
                )
                for d, peer in enumerate(peers)
            ]
            for copy in copies:
                copy.start()
            for copy in copies:
                copy.wait_send()
            local.wait()

    for slot in range(per):

        @pl.when(row != col * per + slot)
        def _():
            pltpu.make_async_remote_copy(
                src_ref=x_ref,
                dst_ref=o_ref.at[slot],
                send_sem=send.at[0],
                recv_sem=recv.at[slot],
                device_id=peers[0],
                device_id_type=MESH,
            ).wait_recv()


def key_tile(packed, n_pb, n_ka):
    per = n_pb // n_ka
    return pl.pallas_call(
        functools.partial(key_tile_kernel, n_pb, n_ka),
        out_shape=jax.ShapeDtypeStruct((per,) + packed.shape, packed.dtype),
        in_specs=[pl.BlockSpec(memory_space=pltpu.VMEM)],
        out_specs=pl.BlockSpec(memory_space=pltpu.VMEM),
        scratch_shapes=[
            pltpu.SemaphoreType.DMA((n_pb - 1,)),
            pltpu.SemaphoreType.DMA((per,)),
            pltpu.SemaphoreType.DMA,
        ],
        compiler_params=pltpu.CompilerParams(collective_id=0, has_side_effects=True),
    )(packed)


def exchange_kernel(n_ka, sums_ref, stats_ref, sums_out, stats_out, send, recv, own):
    me = lax.axis_index("ka")
    peers = [lax.rem(me + d, n_ka) for d in range(1, n_ka)]
    greet([{"ka": peer} for peer in peers])
    copies = []
    for d, peer in enumerate(peers):
        for part, (source, target) in enumerate(((sums_ref, sums_out), (stats_ref, stats_out))):
            copy = pltpu.make_async_remote_copy(
                src_ref=source.at[peer],
                dst_ref=target.at[me],
                send_sem=send.at[2 * d + part],
                recv_sem=recv.at[2 * d + part],
                device_id={"ka": peer},
                device_id_type=MESH,
            )
            copy.start()
            copies.append(copy)
    for part, (source, target) in enumerate(((sums_ref, sums_out), (stats_ref, stats_out))):
        copy = pltpu.make_async_copy(source.at[me], target.at[me], own.at[part])
        copy.start()
        copies.append(copy)
    for copy in copies:
        copy.wait()


def exchange(sums, stats, n_ka):
    return pl.pallas_call(
        functools.partial(exchange_kernel, n_ka),
        out_shape=(
            jax.ShapeDtypeStruct(sums.shape, sums.dtype),
            jax.ShapeDtypeStruct(stats.shape, stats.dtype),
        ),
        in_specs=[pl.BlockSpec(memory_space=pltpu.VMEM)] * 2,
        out_specs=(pl.BlockSpec(memory_space=pltpu.VMEM),) * 2,
        scratch_shapes=[
            pltpu.SemaphoreType.DMA((2 * n_ka - 2,)),
            pltpu.SemaphoreType.DMA((2 * n_ka - 2,)),
            pltpu.SemaphoreType.DMA((2,)),
        ],
        compiler_params=pltpu.CompilerParams(collective_id=1, has_side_effects=True),
    )(sums, stats)


def gather_kernel(n_pb, n_ka, x_ref, o_ref, send, recv, own):
    row, col = lax.axis_index("pb"), lax.axis_index("ka")
    along_pb = [{"pb": lax.rem(row + d, n_pb)} for d in range(1, n_pb)]
    along_ka = [{"ka": lax.rem(col + d, n_ka)} for d in range(1, n_ka)]
    greet(along_pb + along_ka)
    copies = [pltpu.make_async_copy(x_ref, o_ref.at[col, row], own)] + [
        pltpu.make_async_remote_copy(
            src_ref=x_ref,
            dst_ref=o_ref.at[col, row],
            send_sem=send.at[d],
            recv_sem=recv.at[d],
            device_id=peer,
            device_id_type=MESH,
        )
        for d, peer in enumerate(along_pb)
    ]
    for copy in copies:
        copy.start()
    for copy in copies:
        copy.wait()
    copies = [
        pltpu.make_async_remote_copy(
            src_ref=o_ref.at[col],
            dst_ref=o_ref.at[col],
            send_sem=send.at[n_pb - 1 + d],
            recv_sem=recv.at[n_pb - 1 + d],
            device_id=peer,
            device_id_type=MESH,
        )
        for d, peer in enumerate(along_ka)
    ]
    for copy in copies:
        copy.start()
    for copy in copies:
        copy.wait()


def gather_rows(x, n_pb, n_ka):
    out = pl.pallas_call(
        functools.partial(gather_kernel, n_pb, n_ka),
        out_shape=jax.ShapeDtypeStruct((n_ka, n_pb) + x.shape, x.dtype),
        in_specs=[pl.BlockSpec(memory_space=pltpu.VMEM)],
        out_specs=pl.BlockSpec(memory_space=pltpu.VMEM),
        scratch_shapes=[
            pltpu.SemaphoreType.DMA((n_pb + n_ka - 2,)),
            pltpu.SemaphoreType.DMA((n_pb + n_ka - 2,)),
            pltpu.SemaphoreType.DMA,
        ],
        compiler_params=pltpu.CompilerParams(collective_id=2, has_side_effects=True),
    )(x)
    return jnp.transpose(out, (1, 0, 2, 3)).reshape(-1, x.shape[-1])


def edge_kernel(
    pair_ref, row_ref, key_ref, live_row, live_key, first, second, third, bias, scale, o_ref
):
    rows, keys, width = pair_ref.shape
    pair = pair_ref[...].reshape(rows * keys, width)
    hidden = jnp.dot(pair, first[...], preferred_element_type=jnp.float32)
    hidden = hidden.reshape(rows, keys, -1) + row_ref[...][:, None, :] + key_ref[...][None]
    hidden = jnp.maximum(hidden, 0.0).astype(jnp.bfloat16).reshape(rows * keys, -1)
    middle = jnp.dot(hidden, second[...], preferred_element_type=jnp.float32) + bias[...]
    middle = jnp.maximum(middle, 0.0).astype(jnp.bfloat16)
    result = pair.astype(jnp.float32) + jnp.dot(
        middle, third[...], preferred_element_type=jnp.float32
    )
    normed = layer_norm(result, scale[...]).reshape(rows, keys, width)
    live = live_row[...][:, None, :] * live_key[...][None]
    o_ref[...] = (normed * live).astype(o_ref.dtype)


def edge_transition(pair_rep, row_part, key_part, mask_rows, mask_keys, mats, bias, scale):
    rows, keys, width = pair_rep.shape
    step = 8
    live_row = jnp.broadcast_to(mask_rows.astype(jnp.float32)[:, None], (rows, width))
    live_key = jnp.broadcast_to(mask_keys.astype(jnp.float32)[:, None], (keys, width))

    def whole(array):
        return pl.BlockSpec(array.shape, lambda i: (0, 0))

    flat = [live_key, *mats, bias[None], scale[None]]
    return pl.pallas_call(
        edge_kernel,
        grid=(rows // step,),
        out_shape=jax.ShapeDtypeStruct(pair_rep.shape, jnp.bfloat16),
        in_specs=[
            pl.BlockSpec((step, keys, width), lambda i: (i, 0, 0)),
            pl.BlockSpec((step, row_part.shape[1]), lambda i: (i, 0)),
            whole(key_part),
            pl.BlockSpec((step, width), lambda i: (i, 0)),
        ]
        + [whole(array) for array in flat],
        out_specs=pl.BlockSpec((step, keys, width), lambda i: (i, 0, 0)),
    )(pair_rep, row_part, key_part, live_row, *flat)


def finish_rows(
    row_total,
    scalar_acc,
    pair_acc,
    point_acc,
    rotation,
    offset,
    states,
    output_weight,
    attention_scales,
):
    inverse = 1.0 / row_total
    scalar_out = scalar_acc * inverse[..., None]
    pair_out = pair_acc * inverse[..., None]
    point_global = point_acc * inverse[..., None, None]
    features = ipa_features(scalar_out, pair_out, point_global, rotation, offset).astype(
        jnp.bfloat16
    )
    return layer_norm(
        states + jnp.dot(features, output_weight, preferred_element_type=jnp.float32),
        attention_scales,
    )


def on_device(
    node_states,
    frames,
    edge_states,
    chain_number,
    residue_index,
    padding_mask,
    query_weight,
    key_weight,
    value_weight,
    point_query,
    point_key,
    point_value,
    bias_weight,
    point_gamma,
    relpos_table,
    output_weight,
    attention_scales,
    layer_project,
    layer_output,
    layer_expand,
    layer_shrink,
    layer_scales,
    frame_weight,
    node_to_edge,
    edge_first,
    edge_second,
    edge_third,
    edge_biases,
    edge_scales,
):
    row_count = node_states.shape[0]
    key_count = edge_states.shape[1]
    row_first = lax.axis_index("pb") * row_count
    key_first = lax.axis_index("ka") * key_count
    n_pb, n_ka = lax.axis_size("pb"), lax.axis_size("ka")
    packed = jnp.concatenate([node_states, jnp.transpose(frames)], axis=1).astype(jnp.bfloat16)
    packed = jnp.pad(packed, ((0, 0), (0, -packed.shape[1] % 128)))
    tile = key_tile(packed, n_pb, n_ka).reshape(key_count, -1)
    key_input = tile[:, :C_S]
    key_frames = jnp.transpose(tile[:, C_S : C_S + 12].astype(jnp.float32))
    chain_rows = lax.dynamic_slice_in_dim(chain_number, row_first, row_count, 0)
    chain_keys = lax.dynamic_slice_in_dim(chain_number, key_first, key_count, 0)
    index_rows = lax.dynamic_slice_in_dim(residue_index, row_first, row_count, 0)
    index_keys = lax.dynamic_slice_in_dim(residue_index, key_first, key_count, 0)
    mask_rows = lax.dynamic_slice_in_dim(padding_mask, row_first, row_count, 0)
    mask_keys = lax.dynamic_slice_in_dim(padding_mask, key_first, key_count, 0)
    rotation, offset = frame_parts(frames)
    key_rotation, key_offset = frame_parts(key_frames)
    row_input = node_states.astype(jnp.bfloat16)
    queries = head_split(
        jnp.dot(row_input, query_weight, preferred_element_type=jnp.float32).astype(jnp.bfloat16),
        HD,
    )
    key_vectors = head_split(
        jnp.dot(key_input, key_weight, preferred_element_type=jnp.float32).astype(jnp.bfloat16), HD
    )
    value_vectors = head_split(
        jnp.dot(key_input, value_weight, preferred_element_type=jnp.float32).astype(jnp.bfloat16),
        HD,
    )
    query_places = place_points(row_input, point_query, rotation, offset, QKP)
    key_places = place_points(key_input, point_key, key_rotation, key_offset, QKP)
    value_places = place_points(key_input, point_value, key_rotation, key_offset, VP)
    bins = relative_bins(chain_rows, index_rows, chain_keys, index_keys)
    onehot = (bins[:, :, None] == jnp.arange(RELBINS, dtype=jnp.int32)).astype(jnp.float32)
    relative = jnp.dot(onehot.reshape(-1, RELBINS), relpos_table, precision=HIGHEST).reshape(
        row_count, key_count, -1
    )
    pair_rep = (edge_states.astype(jnp.float32) + relative).astype(jnp.bfloat16)
    logits = point_logits(
        queries, key_vectors, query_places, key_places, pair_rep, bias_weight, point_gamma
    )
    key_valid = (mask_keys == 1)[None, None, :]
    masked = jnp.where(key_valid, logits, NEG_FILL)
    local_top = jnp.max(masked, axis=-1)
    weights = jnp.where(key_valid, jnp.exp(masked - local_top[..., None]), 0.0)
    local_total = jnp.sum(weights, axis=-1)
    scalar_acc = jnp.einsum(
        "hij,jhd->hid", weights, value_vectors.astype(jnp.float32), precision=HIGHEST
    )
    pair_acc = jnp.einsum("hij,ijc->hic", weights, pair_rep.astype(jnp.float32), precision=HIGHEST)
    point_acc = jnp.einsum("hij,jhcp->hicp", weights, value_places, precision=HIGHEST)
    part = row_count // n_ka
    sums = jnp.concatenate(
        [
            jnp.transpose(scalar_acc, (1, 0, 2)).reshape(row_count, -1),
            jnp.transpose(pair_acc, (1, 0, 2)).reshape(row_count, -1),
            jnp.transpose(point_acc, (1, 0, 2, 3)).reshape(row_count, -1),
        ],
        axis=1,
    ).astype(jnp.bfloat16)
    used = sums.shape[1]
    sums = jnp.pad(sums, ((0, 0), (0, -used % 128))).reshape(n_ka, part, -1)
    stats = jnp.concatenate([jnp.transpose(local_top), jnp.transpose(local_total)], axis=1)
    stats = jnp.pad(stats, ((0, 0), (0, -stats.shape[1] % 128))).reshape(n_ka, part, -1)
    sums, stats = exchange(sums, stats, n_ka)
    tops, totals = stats[..., :HEADS], stats[..., HEADS : 2 * HEADS]
    factor = jnp.exp(tops - jnp.max(tops, axis=0))
    row_total = jnp.sum(totals * factor, axis=0)
    channels = pair_rep.shape[-1]
    ends = (HEADS * HD, HEADS * (HD + channels))
    spread = jnp.concatenate(
        [
            jnp.repeat(factor, HD, axis=2),
            jnp.repeat(factor, channels, axis=2),
            jnp.repeat(factor, 3 * VP, axis=2),
        ],
        axis=2,
    )
    merged = jnp.sum(sums[..., :used].astype(jnp.float32) * spread, axis=0)
    part_first = lax.axis_index("ka") * part
    first_states = finish_rows(
        row_total,
        merged[:, : ends[0]].reshape(part, HEADS, HD),
        merged[:, ends[0] : ends[1]].reshape(part, HEADS, channels),
        merged[:, ends[1] :].reshape(part, HEADS, 3, VP),
        lax.dynamic_slice_in_dim(rotation, part_first, part, 0),
        lax.dynamic_slice_in_dim(offset, part_first, part, 0),
        lax.dynamic_slice_in_dim(node_states, part_first, part, 0),
        output_weight,
        attention_scales,
    )
    every_valid = padding_mask == 1
    whole_states = gather_rows(first_states.astype(jnp.bfloat16), n_pb, n_ka).astype(
        first_states.dtype
    )
    for layer_number in range(LAYERS):
        projected = jnp.dot(
            whole_states.astype(jnp.bfloat16),
            layer_project[layer_number],
            preferred_element_type=jnp.float32,
        ).astype(jnp.bfloat16)
        whole_states = encoder_core(
            whole_states,
            projected[:, :C_S],
            projected[:, C_S:],
            every_valid,
            layer_output[layer_number],
            layer_expand[layer_number],
            layer_shrink[layer_number],
            layer_scales[layer_number],
        )
    second_states = lax.dynamic_slice_in_dim(whole_states, row_first, row_count, 0)
    key_second = lax.dynamic_slice_in_dim(whole_states, key_first, key_count, 0)
    frames_out = update_frames(second_states, frames, frame_weight)
    row_project = jnp.dot(
        second_states.astype(jnp.bfloat16), node_to_edge[:, :EH], preferred_element_type=jnp.float32
    )
    key_project = jnp.dot(
        key_second.astype(jnp.bfloat16), node_to_edge[:, EH:], preferred_element_type=jnp.float32
    )
    edges_out = edge_transition(
        pair_rep,
        row_project,
        key_project + edge_biases[0],
        mask_rows,
        mask_keys,
        (edge_first, edge_second, edge_third),
        edge_biases[1],
        edge_scales,
    )
    return (second_states, frames_out, edges_out)


def solution(mesh):
    placed = (
        P("pb", None),
        P(None, "pb"),
        P("pb", "ka", None),
        P(),
        P(),
        P(),
        P(),
        P(),
        P(),
        P(),
        P(),
        P(),
        P(),
        P(),
        P(),
        P(),
        P(),
        P(),
        P(),
        P(),
        P(),
        P(),
        P(),
        P(),
        P(),
        P(),
        P(),
        P(),
        P(),
    )
    return jax.shard_map(
        on_device,
        mesh=mesh,
        in_specs=placed,
        out_specs=(P("pb", None), P(None, "pb"), P("pb", "ka", None)),
        check_vma=False,
    )
```

profile of v0, /device:TPU:1, one launch (start us, length us, event | category | flops | bytes accessed | tf_op | source)
XLA Modules:
  0.0 132.7 jit_solution(2584401642835334647)
XLA Ops:
  3.1 8.4 %shard_map.292 = bf16[2,64,384]{2,1,0:T(8,128)(2,1)} custom-call(bf16[64,384]{1,0:T(8,128)(2,1)} %fusion.123.x_ref), custom_call_target="tpu_custom_call" | custom-call | tf_op jit(solution)/shard_map/pallas_call | solution.py:225
  11.5 1.2 fusion.124
  12.7 1.9 %copy.148 = f32[128,8,3,12]{3,2,1,0:T(4,128)} copy(f32[128,8,3,12]{0,3,2,1:T(8,128)S(1)} %reshape.282) | data formatting | bytes 294912 | tf_op jit(solution)/shard_map/reshape | solution.py:44
  15.0 5.3 %add_bitcast_fusion = f32[128,8,3,12]{3,2,1,0:T(4,128)} fusion(f32[128,8,3,12]{3,2,1,0:T(4,128)} %copy.148, bf16[128,3,3,1]{2,1,3,0:T(4,128)(2,1)S(1)} %copy.170, f32[128,3]{1,0:T(8,128)S(1)} %copy.141), kind=kOutput, calls=%fused_computation.20 | convolution fusion | flops 1363968 | bytes 298752 | tf_op jit(solution)/shard_map/rcd,rhdp->rhcp/dot_general | solution.py:45
  20.4 1.8 %copy.139 = f32[128,8,3,8]{3,2,1,0:T(4,128)} copy(f32[128,8,3,8]{0,3,2,1:T(8,128)S(1)} %bitcast.233) | data formatting | bytes 196608 | tf_op jit(solution)/shard_map/reshape | solution.py:44
  22.3 6.6 %multiply_reduce_fusion = (f32[128,8]{1,0:T(8,128)S(1)}, f32[128,8,3,8]{3,2,1,0:T(4,128)}) fusion(f32[128,3]{1,0:T(8,128)S(1)} %copy.141, f32[128,8,3,8]{3,2,1,0:T(4,128)} %copy.139, bf16[128,3,3,1]{2,1,3,0:T(4,128)(2,1)S(1)} %copy.170), kind=kOutput, calls=%fused_computation.21 | convolution fusion | flops 957440 | bytes 204544 | tf_op jit(solution)/shard_map/rcd,rhdp->rhcp/dot_general | solution.py:45
  30.4 3.5 %multiply_reduce_fusion.1 = (f32[64,8]{1,0:T(8,128)S(1)}, f32[64,8,3,8]{3,2,1,0:T(4,128)}) fusion(f32[64,3]{1,0:T(8,128)S(1)} %copy.136, f32[64,8,3,8]{3,2,1,0:T(4,128)S(1)} %copy.134, f32[64,3,3,1]{2,1,3,0:T(4,128)S(1)} %copy.169), kind=kOutput, calls=%fused_computation.63 | convolution fusion | flops 478720 | bytes 103424 | tf_op jit(solution)/shard_map/rcd,rhdp->rhcp/dot_general | solution.py:45
  34.1 5.4 %fusion.37 = f32[8,64,128]{2,1,0:T(8,128)S(1)} fusion(f32[128,8,3,8]{3,2,1,0:T(4,128)} %get-tuple-element.41, f32[64,8,3,8]{3,2,1,0:T(4,128)} %get-tuple-element.43, f32[8,128]{1,0:T(8,128)S(1)} %copy.142, f32[8,64]{1,0:T(8,128)S(1)} %copy.137, f32[8]{0:T(128)S(1)} %broadcast_multiply_fusion.5), kind=kOutput, calls=%fused_computation.56 | convolution fusion | flops 19136512 | bytes 415776 | tf_op jit(solution)/shard_map/ihcp,jhcp->hij/dot_general | solution.py:65
  39.9 4.6 %add_convert_fusion.pair_ref = bf16[64,128,128]{2,1,0:T(8,128)(2,1)S(1)} fusion(bf16[64,128,128]{2,1,0:T(8,128)(2,1)} %param.31, s32[64,128]{1,0:T(8,128)S(1)} %add_select_fusion, f32[128,128]{1,0:T(8,128)S(1)} %copy-done.13), kind=kOutput, calls=%fused_computation.8 | convolution fusion | flops 1614807040 | bytes 4292608 | tf_op jit(solution)/shard_map/dot_general | solution.py:468
  45.3 1.3 copy-done.4
  48.5 3.1 %fusion.43 = bf16[64,8,3,12]{0,3,2,1:T(8,128)(2,1)S(1)} fusion(f32[128,8,3,12]{3,2,1,0:T(4,128)S(1)} %copy-done.2, f32[8,64,128]{2,1,0:T(8,128)S(1)} %get-tuple-element.15), kind=kOutput, calls=%fused_computation.61 | convolution fusion | flops 28329984 | bytes 446464 | tf_op jit(solution)/shard_map/hij,jhcp->hicp/dot_general | solution.py:484
  51.7 3.3 %convolution_convert_fusion.6 = bf16[64,8,128]{2,1,0:T(8,128)(2,1)S(1)} fusion(bf16[64,128,128]{2,1,0:T(8,128)(2,1)} %copy-done.1, f32[8,64,128]{2,1,0:T(8,128)S(1)} %get-tuple-element.15), kind=kOutput, calls=%fused_computation.58 | convolution fusion | flops 100728832 | bytes 2490368 | tf_op jit(solution)/shard_map/hij,ijc->hic/dot_general | solution.py:483
  55.1 1.5 %convolution_convert_fusion = bf16[128,2048]{1,0:T(8,128)(2,1)S(1)} fusion(bf16[256,2048]{1,0:T(8,128)(2,1)} %param.37, bf16[128,384]{1,0:T(8,128)(2,1)S(1)} %bitcast.225), kind=kOutput, calls=%fused_computation.13 | convolution fusion | flops 134479872 | bytes 1638400 | tf_op jit(solution)/shard_map/dot_general | solution.py:460
  58.5 12.7 %shard_map.293 = (bf16[4,16,3456]{2,1,0:T(8,128)(2,1)}, f32[4,16,128]{2,1,0:T(8,128)}) custom-call(bf16[4,16,3456]{2,1,0:T(8,128)(2,1)} %bitcast.220, f32[4,16,128]{2,1,0:T(8,128)} %bitcast.247), custom_call_target="tpu_custom_call" | custom-call | tf_op jit(solution)/shard_map/pallas_call | solution.py:265
  77.0 1.2 fusion.148
  79.0 12.8 %shard_map.294 = bf16[4,8,16,256]{3,2,1,0:T(8,128)(2,1)} custom-call(bf16[16,256]{1,0:T(8,128)(2,1)} %multiply_convert_fusion.x_ref), custom_call_target="tpu_custom_call" | custom-call | tf_op jit(solution)/shard_map/pallas_call | solution.py:320
  93.7 3.8 %fusion.149 = (f32[4,512]{1,0:T(4,128)S(1)}, f32[4,512,512]{1,2,0:T(8,128)}) fusion(pred[512]{0:T(512)(128)(4,1)S(1)} %broadcast_compare_fusion, bf16[512,4,64]{0,2,1:T(8,128)(2,1)S(1)} %bitcast.240, bf16[512,4,64]{0,2,1:T(8,128)(2,1)S(1)} %bitcast.242), kind=kOutput, calls=%fused_computation.222 | convolution fusion | flops 139461120 | bytes 4727296 | tf_op jit(solution)/shard_map/sub | solution.py:102
  97.5 2.7 %fusion.22 = bf16[4,64,512]{2,1,0:T(8,128)(2,1)S(1)} fusion(bf16[512,4,64]{0,2,1:T(8,128)(2,1)S(1)} %bitcast.237, f32[4,512,512]{1,2,0:T(8,128)} %get-tuple-element.49, f32[4,512]{1,0:T(4,128)S(1)} %get-tuple-element.48), kind=kOutput, calls=%fused_computation.46 | convolution fusion | flops 136445952 | bytes 4726784 | tf_op jit(solution)/shard_map/hij,jhd->ihd/dot_general | solution.py:104
  100.9 1.5 %fusion.151 = (f32[512]{0:T(512)S(1)}, f32[512,256]{1,0:T(8,128)S(1)}) fusion(bf16[2,256,256]{2,1,0:T(8,128)(2,1)} %param.49, f32[512,256]{1,0:T(8,128)S(1)} %get-tuple-element.51, f32[256]{0:T(256)S(1)} %bitcast.258, f32[512]{0:T(512)S(1)} %add_rsqrt_fusion.3, f32[512]{0:T(512)S(1)} %broadcast_multiply_fusion.3, bf16[2,256,256]{2,1,0:T(8,128)(2,1)} %param.48), kind=kOutput, calls=%fused_computation.224 | convolution fusion | flops 135659008 | bytes 1847296 | tf_op jit(solution)/shard_map/dot_general | solution.py:115
  102.7 1.5 %convolution_convert_fusion.3 = bf16[512,768]{1,0:T(8,128)(2,1)S(1)} fusion(bf16[2,256,768]{2,1,0:T(8,128)(2,1)} %param.46, f32[512,256]{1,0:T(8,128)S(1)} %get-tuple-element.53, f32[256]{0:T(256)S(1)} %bitcast.254, f32[512]{0:T(512)S(1)} %add_rsqrt_fusion.2, f32[512]{0:T(512)S(1)} %broadcast_multiply_fusion.2), kind=kOutput, calls=%fused_computation.32 | convolution fusion | flops 202244096 | bytes 1709056 | tf_op jit(solution)/shard_map/dot_general | solution.py:530
  105.4 3.8 %fusion.156 = (f32[4,512]{1,0:T(4,128)S(1)}, f32[4,512,512]{1,2,0:T(8,128)}) fusion(pred[512]{0:T(512)(128)(4,1)S(1)} %broadcast_compare_fusion, bf16[512,4,64]{0,2,1:T(8,128)(2,1)S(1)} %bitcast.239, bf16[512,4,64]{0,2,1:T(8,128)(2,1)S(1)} %bitcast.241), kind=kOutput, calls=%fused_computation.225 | convolution fusion | flops 139461120 | bytes 4727296 | tf_op jit(solution)/shard_map/sub | solution.py:102
  109.2 2.7 %fusion.21 = bf16[4,64,512]{2,1,0:T(8,128)(2,1)S(1)} fusion(bf16[512,4,64]{0,2,1:T(8,128)(2,1)S(1)} %bitcast.238, f32[4,512,512]{1,2,0:T(8,128)} %get-tuple-element.55, f32[4,512]{1,0:T(4,128)S(1)} %get-tuple-element.54), kind=kOutput, calls=%fused_computation.45 | convolution fusion | flops 136445952 | bytes 4726784 | tf_op jit(solution)/shard_map/hij,jhd->ihd/dot_general | solution.py:104
  112.6 1.5 %fusion.158 = (f32[512]{0:T(512)S(1)}, f32[512,256]{1,0:T(8,128)S(1)}) fusion(bf16[2,256,256]{2,1,0:T(8,128)(2,1)} %param.49, f32[512,256]{1,0:T(8,128)S(1)} %get-tuple-element.57, f32[256]{0:T(256)S(1)} %bitcast.257, f32[512]{0:T(512)S(1)} %add_rsqrt_fusion.1, f32[512]{0:T(512)S(1)} %broadcast_multiply_fusion.1, bf16[2,256,256]{2,1,0:T(8,128)(2,1)} %param.48), kind=kOutput, calls=%fused_computation.227 | convolution fusion | flops 135659008 | bytes 1847296 | tf_op jit(solution)/shard_map/dot_general | solution.py:115
  120.3 12.3 %shard_map.295 = bf16[64,128,128]{2,1,0:T(8,128)(2,1)} custom-call(bf16[64,128,128]{2,1,0:T(8,128)(2,1)} %copy-done.1, f32[64,384]{1,0:T(8,128)} %fusion.98.row_ref, f32[128,384]{1,0:T(8,128)} %convolution_add_fusion.5.key_ref, f32[64,128]{1,0:T(8,128)} %broadcast_in_dim.120.live_row, f32[128,128]{1,0:T(8,128)} %broadcast_in_dim.121.live_key, ...), custom_call_target="tpu_custom_call" | custom-call | tf_op jit(solution)/shard_map/pallas_call | solution.py:363
  (170 shorter events, 26.7 us)
Async XLA Ops:
  0.6 76.3 %copy-start = (bf16[3456,256]{1,0:T(8,128)(2,1)S(1)}, bf16[3456,256]{1,0:T(8,128)(2,1)}, u32[]{:S(2)}) copy-start(bf16[3456,256]{1,0:T(8,128)(2,1)} %param.44) | copy-start | bytes 5308420
  11.5 3.1 %copy-start.3 = (bf16[2,64,384]{2,1,0:T(8,128)(2,1)S(1)}, bf16[2,64,384]{2,1,0:T(8,128)(2,1)}, u32[]{:S(2)}) copy-start(bf16[2,64,384]{2,1,0:T(8,128)(2,1)} %shard_map.292) | copy-start | bytes 294916
  15.0 5.3 %copy-start.12 = (bf16[256,192]{0,1:T(8,128)(2,1)S(1)}, bf16[256,192]{0,1:T(8,128)(2,1)}, u32[]{:S(2)}) copy-start(bf16[256,192]{0,1:T(8,128)(2,1)} %param.39) | copy-start | bytes 294916
  22.3 6.6 %copy-start.14 = (f32[12,64]{1,0:T(8,128)S(1)}, f32[12,64]{1,0:T(8,128)}, u32[]{:S(2)}) copy-start(f32[12,64]{1,0:T(8,128)} %param.30) | copy-start | bytes 9220
  22.3 6.7 %copy-start.11 = (bf16[256,192]{0,1:T(8,128)(2,1)S(1)}, bf16[256,192]{0,1:T(8,128)(2,1)}, u32[]{:S(2)}) copy-start(bf16[256,192]{0,1:T(8,128)(2,1)} %param.38) | copy-start | bytes 294916
  28.8 5.2 %copy-start.23 = (f32[8]{0:T(128)S(1)}, f32[8]{0:T(128)}, u32[]{:S(2)}) copy-start(f32[8]{0:T(128)} %param.42) | copy-start | bytes 100
  30.4 9.1 %copy-start.21 = (s32[512]{0:T(512)S(1)}, s32[512]{0:T(512)}, u32[]{:S(2)}) copy-start(s32[512]{0:T(512)} %param.33) | copy-start | bytes 6148
  30.4 9.3 %copy-start.22 = (s32[512]{0:T(512)S(1)}, s32[512]{0:T(512)}, u32[]{:S(2)}) copy-start(s32[512]{0:T(512)} %param.32) | copy-start | bytes 6148
  30.4 9.5 %copy-start.13 = (f32[128,128]{1,0:T(8,128)S(1)}, f32[128,128]{1,0:T(8,128)}, u32[]{:S(2)}) copy-start(f32[128,128]{1,0:T(8,128)} %param.43) | copy-start | bytes 196612
  39.9 4.7 %copy-start.19 = (bf16[128,8]{0,1:T(8,128)(2,1)S(1)}, bf16[128,8]{0,1:T(8,128)(2,1)}, u32[]{:S(2)}) copy-start(bf16[128,8]{0,1:T(8,128)(2,1)} %param.41) | copy-start | bytes 6148
  44.6 2.6 %copy-start.1 = (bf16[64,128,128]{2,1,0:T(8,128)(2,1)}, bf16[64,128,128]{2,1,0:T(8,128)(2,1)S(1)}, u32[]{:S(2)}) copy-start(bf16[64,128,128]{2,1,0:T(8,128)(2,1)S(1)} %add_convert_fusion.pair_ref) | copy-start | bytes 6291460
  44.6 2.0 %copy-start.4 = (bf16[256,2048]{1,0:T(8,128)(2,1)S(1)}, bf16[256,2048]{1,0:T(8,128)(2,1)}, u32[]{:S(2)}) copy-start(bf16[256,2048]{1,0:T(8,128)(2,1)} %param.36) | copy-start | bytes 3145732
  44.6 2.3 %copy-start.5 = (bf16[256,2048]{1,0:T(8,128)(2,1)S(1)}, bf16[256,2048]{1,0:T(8,128)(2,1)}, u32[]{:S(2)}) copy-start(bf16[256,2048]{1,0:T(8,128)(2,1)} %param.35) | copy-start | bytes 3145732
  44.6 2.6 %copy-start.18 = (s32[512]{0:T(512)S(1)}, s32[512]{0:T(512)}, u32[]{:S(2)}) copy-start(s32[512]{0:T(512)} %param.34) | copy-start | bytes 6148
  46.9 1.6 %copy-start.2 = (f32[128,8,3,12]{3,2,1,0:T(4,128)S(1)}, f32[128,8,3,12]{3,2,1,0:T(4,128)}, u32[]{:S(2)}) copy-start(f32[128,8,3,12]{3,2,1,0:T(4,128)} %add_bitcast_fusion) | copy-start | bytes 442372
  74.9 3.4 %copy-start.20 = (f32[256]{0:T(256)S(1)}, f32[256]{0:T(256)}, u32[]{:S(2)}) copy-start(f32[256]{0:T(256)} %param.45) | copy-start | bytes 3076
  75.3 17.6 %copy-start.6 = (bf16[2,256,768]{2,1,0:T(8,128)(2,1)S(1)}, bf16[2,256,768]{2,1,0:T(8,128)(2,1)}, u32[]{:S(2)}) copy-start(bf16[2,256,768]{2,1,0:T(8,128)(2,1)} %param.46) | copy-start | bytes 2359300
  97.5 2.7 %copy-start.9 = (bf16[2,256,256]{2,1,0:T(8,128)(2,1)S(1)}, bf16[2,256,256]{2,1,0:T(8,128)(2,1)}, u32[]{:S(2)}) copy-start(bf16[2,256,256]{2,1,0:T(8,128)(2,1)} %param.47) | copy-start | bytes 786436
  97.5 3.1 %copy-start.16 = (f32[2,2,256]{2,1,0:T(2,128)S(1)}, f32[2,2,256]{2,1,0:T(2,128)}, u32[]{:S(2)}) copy-start(f32[2,2,256]{2,1,0:T(2,128)} %param.50) | copy-start | bytes 12292
  105.4 3.8 %copy-start.10 = (bf16[512,256]{0,1:T(8,128)(2,1)S(1)}, bf16[512,256]{0,1:T(8,128)(2,1)}, u32[]{:S(2)}) copy-start(bf16[512,256]{0,1:T(8,128)(2,1)} %copy.161) | copy-start | bytes 786436
  112.3 2.3 %copy-start.15 = (f32[256,6]{0,1:T(8,128)S(1)}, f32[256,6]{0,1:T(8,128)}, u32[]{:S(2)}) copy-start(f32[256,6]{0,1:T(8,128)} %param.51) | copy-start | bytes 18436
  112.6 4.0 %copy-start.8 = (bf16[256,768]{1,0:T(8,128)(2,1)S(1)}, bf16[256,768]{1,0:T(8,128)(2,1)}, u32[]{:S(2)}) copy-start(bf16[256,768]{1,0:T(8,128)(2,1)} %param.52) | copy-start | bytes 1179652
  112.6 4.8 %copy-start.17 = (f32[2,384]{1,0:T(2,128)S(1)}, f32[2,384]{1,0:T(2,128)}, u32[]{:S(2)}) copy-start(f32[2,384]{1,0:T(2,128)} %param.56) | copy-start | bytes 9220
  114.7 18.0 %copy-start.7 = (f32[64,256]{1,0:T(8,128)}, f32[64,256]{1,0:T(8,128)S(1)}, u32[]{:S(2)}) copy-start(f32[64,256]{1,0:T(8,128)S(1)} %constant_dynamic-slice_fusion) | copy-start | bytes 196612
where the time goes:
time: 134 us; the launch traced here: 133 us
  matrix products  59.9 us (45%)
  Pallas kernels  46.2 us (34%)
  local copies, waits for them, and re-layouts  15.6 us (12%)
  other arithmetic  9.38 us (7%)
  between operations  1.45 us (1%)
    dot_general x3, matrix products, place_points(): placed = jnp.einsum('rcd,rhdp->rhcp', rotation, local, precision=HIGHEST)  15.4 us
    pallas_call x1, Pallas kernels, gather_rows(): pl.pallas_call(functools.partial(gather_kernel, n_pb, n_ka), out_shape=ja...  12.8 us
    pallas_call x1, Pallas kernels, exchange(): pl.pallas_call(functools.partial(exchange_kernel, n_ka), out_shape=(jax.S...  12.7 us
    pallas_call x1, Pallas kernels, edge_transition(): pl.pallas_call(edge_kernel, grid=(rows // step,), out_shape=jax.ShapeDtyp...  12.3 us
    pallas_call x1, Pallas kernels, key_tile(): pl.pallas_call(functools.partial(key_tile_kernel, n_pb, n_ka), out_shape=...  8.39 us
    sub x2, matrix products, encoder_core(): weights = jnp.where(valid[None, None, :], jnp.exp(masked - row_top), 0.0)  7.65 us
    dot_general x1, matrix products, point_logits(): jnp.einsum('ihcp,jhcp->hij', query_places, key_places, precision=HIGHEST)  5.44 us
    dot_general x2, matrix products, encoder_core(): jnp.einsum('hij,jhd->ihd', attention, value_vectors, preferred_element_ty...  5.4 us

commit v1 on v0

--- a/solution.py
+++ b/solution.py
@@ -3,6 +3,7 @@
 
 import jax
 import jax.numpy as jnp
+import numpy as np
 from jax import lax
 from jax.experimental import pallas as pl
 from jax.experimental.pallas import tpu as pltpu
@@ -39,11 +40,54 @@
     return matrix.reshape(matrix.shape[0], -1, width)
 
 
+def lane_parts(count):
+    width = HEADS * 3 * count
+    padded = -(-width // 128) * 128
+    lane = np.arange(padded)
+    real = lane < width
+    head, comp, point = lane // (3 * count), lane // count % 3, lane % count
+    return padded, real, head, comp, point
+
+
+def pick(sources, size, dtype):
+    sources = jnp.asarray(sources, jnp.int32)
+    return (jnp.arange(size, dtype=jnp.int32)[:, None] == sources[None, :]).astype(dtype)
+
+
+def component_copies(count, size, dtype):
+    padded, real, head, comp, point = lane_parts(count)
+    copies = [np.where(real, (head * 3 + d) * count + point, -1) for d in range(3)]
+    return pick(np.concatenate(copies), size, dtype)
+
+
+def rotation_lanes(rotation, count, inverse):
+    padded, real, head, comp, point = lane_parts(count)
+    entries = [np.where(real, d * 3 + comp if inverse else comp * 3 + d, -1) for d in range(3)]
+    return jnp.dot(
+        rotation, pick(np.concatenate(entries), 9, jnp.float32), precision=HIGHEST
+    )
+
+
+def offset_lanes(offset, count):
+    padded, real, head, comp, point = lane_parts(count)
+    return jnp.dot(offset, pick(np.where(real, comp, -1), 3, jnp.float32), precision=HIGHEST)
+
+
+def head_lanes(count):
+    padded, real, head, comp, point = lane_parts(count)
+    return pick(np.where(real, head, -1), HEADS, jnp.float32)
+
+
+def add_thirds(values):
+    third = values.shape[1] // 3
+    return values[:, :third] + values[:, third : 2 * third] + values[:, 2 * third :]
+
+
 def place_points(features, weight, rotation, offset, count):
-    local = jnp.dot(features, weight, preferred_element_type=jnp.float32)
-    local = local.reshape(local.shape[0], HEADS, 3, count)
-    placed = jnp.einsum("rcd,rhdp->rhcp", rotation, local, precision=HIGHEST)
-    return placed + offset[:, None, :, None]
+    copies = component_copies(count, weight.shape[1], weight.dtype)
+    spread = jnp.dot(weight, copies, preferred_element_type=jnp.float32).astype(weight.dtype)
+    local = jnp.dot(features, spread, preferred_element_type=jnp.float32)
+    return add_thirds(local * rotation_lanes(rotation, count, False)) + offset_lanes(offset, count)
 
 
 def relative_bins(chain_rows, index_rows, chain_cols, index_cols):
@@ -60,33 +104,40 @@
         "ihd,jhd->hij", queries, key_vectors, preferred_element_type=jnp.float32
     ) / math.sqrt(HD)
     pair_bias = jnp.einsum("ijc,ch->hij", pair_rep, bias_weight, preferred_element_type=jnp.float32)
-    query_square = jnp.sum(query_places * query_places, axis=(2, 3))
-    key_square = jnp.sum(key_places * key_places, axis=(2, 3))
-    cross = jnp.einsum("ihcp,jhcp->hij", query_places, key_places, precision=HIGHEST)
-    distance = (
-        jnp.transpose(query_square)[:, :, None]
-        + jnp.transpose(key_square)[:, None, :]
-        - 2.0 * cross
-    )
+    heads = head_lanes(QKP)
+    query_square = lax.dot_general(
+        heads, query_places * query_places, (((1,), (1,)), ((), ())), precision=HIGHEST
+    )
+    key_square = lax.dot_general(
+        heads, key_places * key_places, (((1,), (1,)), ((), ())), precision=HIGHEST
+    )
+    by_head = (query_places[None] * heads[:, None, :]).reshape(-1, query_places.shape[1])
+    cross = lax.dot_general(
+        by_head, key_places, (((1,), (1,)), ((), ())), precision=HIGHEST
+    ).reshape(HEADS, query_places.shape[0], -1)
+    distance = query_square[:, :, None] + key_square[:, None, :] - 2.0 * cross
     weight_points = math.sqrt(2.0 / (9.0 * QKP))
     return math.sqrt(1.0 / 3.0) * (
         scalar + pair_bias - 0.5 * weight_points * point_gamma[:, None, None] * distance
     )
 
 
-def ipa_features(scalar_out, pair_out, point_global, rotation, offset):
-    moved = point_global - offset[:, None, :, None]
-    local = jnp.einsum("icd,ihcp->ihdp", rotation, moved, precision=HIGHEST)
-    lengths = jnp.sqrt(jnp.sum(local * local, axis=2) + 1e-08)
-    count = scalar_out.shape[0]
+def ipa_features(merged, rotation, offset):
+    points_first = merged.shape[1] - HEADS * 3 * VP
+    padded, real, head, comp, point = lane_parts(VP)
+    point_global = jnp.pad(
+        merged[:, points_first:], ((0, 0), (0, padded - HEADS * 3 * VP))
+    )
+    moved = point_global - offset_lanes(offset, VP)
+    rotated = jnp.dot(
+        moved, component_copies(VP, padded, jnp.float32), precision=HIGHEST
+    ) * rotation_lanes(rotation, VP, True)
+    local = add_thirds(rotated)
+    owner = np.where(real, head * VP + point, -1)
+    same = jnp.transpose(pick(owner, HEADS * VP, jnp.float32))
+    lengths = jnp.sqrt(jnp.dot(local * local, same, precision=HIGHEST) + 1e-08)
     return jnp.concatenate(
-        [
-            scalar_out.reshape(count, -1),
-            pair_out.reshape(count, -1),
-            local.reshape(count, -1),
-            lengths.reshape(count, -1),
-        ],
-        axis=1,
+        [merged[:, :points_first], local[:, : HEADS * 3 * VP], lengths], axis=1
     )
 
 
@@ -375,24 +426,8 @@
     )(pair_rep, row_part, key_part, live_row, *flat)
 
 
-def finish_rows(
-    row_total,
-    scalar_acc,
-    pair_acc,
-    point_acc,
-    rotation,
-    offset,
-    states,
-    output_weight,
-    attention_scales,
-):
-    inverse = 1.0 / row_total
-    scalar_out = scalar_acc * inverse[..., None]
-    pair_out = pair_acc * inverse[..., None]
-    point_global = point_acc * inverse[..., None, None]
-    features = ipa_features(scalar_out, pair_out, point_global, rotation, offset).astype(
-        jnp.bfloat16
-    )
+def finish_rows(merged, rotation, offset, states, output_weight, attention_scales):
+    features = ipa_features(merged, rotation, offset).astype(jnp.bfloat16)
     return layer_norm(
         states + jnp.dot(features, output_weight, preferred_element_type=jnp.float32),
         attention_scales,
@@ -439,15 +474,15 @@
     packed = jnp.pad(packed, ((0, 0), (0, -packed.shape[1] % 128)))
     tile = key_tile(packed, n_pb, n_ka).reshape(key_count, -1)
     key_input = tile[:, :C_S]
-    key_frames = jnp.transpose(tile[:, C_S : C_S + 12].astype(jnp.float32))
+    key_rotation = tile[:, C_S : C_S + 9].astype(jnp.float32)
+    key_offset = tile[:, C_S + 9 : C_S + 12].astype(jnp.float32)
     chain_rows = lax.dynamic_slice_in_dim(chain_number, row_first, row_count, 0)
     chain_keys = lax.dynamic_slice_in_dim(chain_number, key_first, key_count, 0)
     index_rows = lax.dynamic_slice_in_dim(residue_index, row_first, row_count, 0)
     index_keys = lax.dynamic_slice_in_dim(residue_index, key_first, key_count, 0)
     mask_rows = lax.dynamic_slice_in_dim(padding_mask, row_first, row_count, 0)
     mask_keys = lax.dynamic_slice_in_dim(padding_mask, key_first, key_count, 0)
-    rotation, offset = frame_parts(frames)
-    key_rotation, key_offset = frame_parts(key_frames)
+    rotation, offset = jnp.transpose(frames[:9]), jnp.transpose(frames[9:12])
     row_input = node_states.astype(jnp.bfloat16)
     queries = head_split(
         jnp.dot(row_input, query_weight, preferred_element_type=jnp.float32).astype(jnp.bfloat16),
@@ -464,10 +499,15 @@
     key_places = place_points(key_input, point_key, key_rotation, key_offset, QKP)
     value_places = place_points(key_input, point_value, key_rotation, key_offset, VP)
     bins = relative_bins(chain_rows, index_rows, chain_keys, index_keys)
-    onehot = (bins[:, :, None] == jnp.arange(RELBINS, dtype=jnp.int32)).astype(jnp.float32)
-    relative = jnp.dot(onehot.reshape(-1, RELBINS), relpos_table, precision=HIGHEST).reshape(
-        row_count, key_count, -1
-    )
+    onehot = (bins[:, :, None] == jnp.arange(RELBINS, dtype=jnp.int32)).astype(jnp.bfloat16)
+    onehot = onehot.reshape(-1, RELBINS)
+    table_top = lax.reduce_precision(relpos_table, 8, 7)
+    table_high = table_top.astype(jnp.bfloat16)
+    table_low = (relpos_table - table_top).astype(jnp.bfloat16)
+    relative = (
+        jnp.dot(onehot, table_high, preferred_element_type=jnp.float32)
+        + jnp.dot(onehot, table_low, preferred_element_type=jnp.float32)
+    ).reshape(row_count, key_count, -1)
     pair_rep = (edge_states.astype(jnp.float32) + relative).astype(jnp.bfloat16)
     logits = point_logits(
         queries, key_vectors, query_places, key_places, pair_rep, bias_weight, point_gamma
@@ -477,17 +517,21 @@
     local_top = jnp.max(masked, axis=-1)
     weights = jnp.where(key_valid, jnp.exp(masked - local_top[..., None]), 0.0)
     local_total = jnp.sum(weights, axis=-1)
+    rounded = weights.astype(jnp.bfloat16)
     scalar_acc = jnp.einsum(
-        "hij,jhd->hid", weights, value_vectors.astype(jnp.float32), precision=HIGHEST
-    )
-    pair_acc = jnp.einsum("hij,ijc->hic", weights, pair_rep.astype(jnp.float32), precision=HIGHEST)
-    point_acc = jnp.einsum("hij,jhcp->hicp", weights, value_places, precision=HIGHEST)
+        "hij,jhd->ihd", rounded, value_vectors, preferred_element_type=jnp.float32
+    )
+    pair_acc = jnp.einsum("hij,ijc->ihc", rounded, pair_rep, preferred_element_type=jnp.float32)
+    point_all = jnp.dot(
+        weights.reshape(-1, key_count), value_places, precision=HIGHEST
+    ).reshape(HEADS, row_count, -1)
+    point_acc = jnp.sum(point_all * head_lanes(VP)[:, None, :], axis=0)
     part = row_count // n_ka
     sums = jnp.concatenate(
         [
-            jnp.transpose(scalar_acc, (1, 0, 2)).reshape(row_count, -1),
-            jnp.transpose(pair_acc, (1, 0, 2)).reshape(row_count, -1),
-            jnp.transpose(point_acc, (1, 0, 2, 3)).reshape(row_count, -1),
+            scalar_acc.reshape(row_count, -1),
+            pair_acc.reshape(row_count, -1),
+            point_acc[:, : HEADS * 3 * VP],
         ],
         axis=1,
     ).astype(jnp.bfloat16)
@@ -498,9 +542,8 @@
     sums, stats = exchange(sums, stats, n_ka)
     tops, totals = stats[..., :HEADS], stats[..., HEADS : 2 * HEADS]
     factor = jnp.exp(tops - jnp.max(tops, axis=0))
-    row_total = jnp.sum(totals * factor, axis=0)
+    factor = factor / jnp.sum(totals * factor, axis=0)
     channels = pair_rep.shape[-1]
-    ends = (HEADS * HD, HEADS * (HD + channels))
     spread = jnp.concatenate(
         [
             jnp.repeat(factor, HD, axis=2),
@@ -512,10 +555,7 @@
     merged = jnp.sum(sums[..., :used].astype(jnp.float32) * spread, axis=0)
     part_first = lax.axis_index("ka") * part
     first_states = finish_rows(
-        row_total,
-        merged[:, : ends[0]].reshape(part, HEADS, HD),
-        merged[:, ends[0] : ends[1]].reshape(part, HEADS, channels),
-        merged[:, ends[1] :].reshape(part, HEADS, 3, VP),
+        merged,
         lax.dynamic_slice_in_dim(rotation, part_first, part, 0),
         lax.dynamic_slice_in_dim(offset, part_first, part, 0),
         lax.dynamic_slice_in_dim(node_states, part_first, part, 0),
@@ -527,23 +567,37 @@
         first_states.dtype
     )
     for layer_number in range(LAYERS):
-        projected = jnp.dot(
+        projection = layer_project[layer_number]
+        key_value = jnp.dot(
             whole_states.astype(jnp.bfloat16),
-            layer_project[layer_number],
+            projection[:, C_S:],
+            preferred_element_type=jnp.float32,
+        ).astype(jnp.bfloat16)
+        if layer_number == LAYERS - 1:
+            whole_states = jnp.concatenate(
+                [
+                    lax.dynamic_slice_in_dim(whole_states, row_first, row_count, 0),
+                    lax.dynamic_slice_in_dim(whole_states, key_first, key_count, 0),
+                ],
+                axis=0,
+            )
+        query_half = jnp.dot(
+            whole_states.astype(jnp.bfloat16),
+            projection[:, :C_S],
             preferred_element_type=jnp.float32,
         ).astype(jnp.bfloat16)
         whole_states = encoder_core(
             whole_states,
-            projected[:, :C_S],
-            projected[:, C_S:],
+            query_half,
+            key_value,
             every_valid,
             layer_output[layer_number],
             layer_expand[layer_number],
             layer_shrink[layer_number],
             layer_scales[layer_number],
         )
-    second_states = lax.dynamic_slice_in_dim(whole_states, row_first, row_count, 0)
-    key_second = lax.dynamic_slice_in_dim(whole_states, key_first, key_count, 0)
+    second_states = whole_states[:row_count]
+    key_second = whole_states[row_count:]
     frames_out = update_frames(second_states, frames, frame_weight)
     row_project = jnp.dot(
         second_states.astype(jnp.bfloat16), node_to_edge[:, :EH], preferred_element_type=jnp.float32

time: 134 us -> 108 us (0.81)
  matrix products: 59.9 us -> 38.4 us
  local copies, waits for them, and re-layouts: 15.6 us -> 10.8 us
    dot_general x14 -> x25, matrix products: 36.4 us -> 17.9 us  [the longest x3 4.36 us: place_points(): local = jnp.dot(features, spread, preferred_element_type=jnp.float32)]
    reshape x9 -> x1, local copies, waits for them, and re-layouts: 5.43 us -> 0.02 us  [on_device(): scalar_acc.reshape(row_count, -1)]
    sub x2, matrix products: 7.65 us -> 5.69 us  [encoder_core(): weights = jnp.where(valid[None, None, :], jnp.exp(masked - row_top), 0.0)]
where the time goes in v1:
time: 108 us; the launch traced here: 107 us
  Pallas kernels  46.3 us (43%)
  matrix products  38.4 us (36%)
  local copies, waits for them, and re-layouts  10.8 us (10%)
  other arithmetic  10 us (9%)
  between operations  1.58 us (1%)
    pallas_call x1, Pallas kernels, gather_rows(): pl.pallas_call(functools.partial(gather_kernel, n_pb, n_ka), out_shape=ja...  12.8 us
    pallas_call x1, Pallas kernels, exchange(): pl.pallas_call(functools.partial(exchange_kernel, n_ka), out_shape=(jax.S...  12.7 us
    pallas_call x1, Pallas kernels, edge_transition(): pl.pallas_call(edge_kernel, grid=(rows // step,), out_shape=jax.ShapeDtyp...  12.3 us
    pallas_call x1, Pallas kernels, key_tile(): pl.pallas_call(functools.partial(key_tile_kernel, n_pb, n_ka), out_shape=...  8.41 us
    sub x2, matrix products, encoder_core(): weights = jnp.where(valid[None, None, :], jnp.exp(masked - row_top), 0.0)  5.69 us
    dot_general x2, matrix products, encoder_core(): jnp.einsum('hij,jhd->ihd', attention, value_vectors, preferred_element_ty...  4.65 us
    dot_general x3, matrix products, place_points(): local = jnp.dot(features, spread, preferred_element_type=jnp.float32)  4.36 us
    dot_general x4, matrix products, offset_lanes(): jnp.dot(offset, pick(np.where(real, comp, -1), 3, jnp.float32), precision...  2.87 us

profile of v1, /device:TPU:1, one launch (start us, length us, event | category | flops | bytes accessed | tf_op | source)
XLA Modules:
  0.0 107.1 jit_solution(8796491648850374875)
XLA Ops:
  4.0 2.2 %fusion.2 = f32[8192,128]{1,0:T(8,128)S(1)} fusion(s32[8192]{0:T(1024)S(1)} %fusion.130, f32[128,128]{1,0:T(8,128)} %param.58), kind=kOutput, calls=%fused_computation.8 | convolution fusion | flops 269516800 | bytes 4292608 | tf_op jit(solution)/shard_map/dot_general | solution.py:508
  6.2 1.3 %convolution_add_fusion = f32[8192,128]{1,0:T(8,128)S(1)} fusion(f32[8192,128]{1,0:T(8,128)S(1)} %fusion.2, s32[8192]{0:T(1024)S(1)} %fusion.130, f32[128,128]{1,0:T(8,128)S(1)} %copy-done.10), kind=kOutput, calls=%fused_computation.2 | convolution fusion | flops 270581760 | bytes 8486912 | tf_op jit(solution)/shard_map/dot_general | solution.py:509
  8.6 1.3 %copy-done.1 = bf16[64,128,128]{2,1,0:T(8,128)(2,1)} copy-done((bf16[64,128,128]{2,1,0:T(8,128)(2,1)}, bf16[64,128,128]{2,1,0:T(8,128)(2,1)S(1)}, u32[]{:S(2)}) %copy-start.1) | copy-done | bytes 2097176
  11.5 8.4 %shard_map.427 = bf16[2,64,384]{2,1,0:T(8,128)(2,1)} custom-call(bf16[64,384]{1,0:T(8,128)(2,1)} %fusion.118.x_ref), custom_call_target="tpu_custom_call" | custom-call | tf_op jit(solution)/shard_map/pallas_call | solution.py:276
  20.0 1.2 %convolution_convert_fusion.1 = bf16[128,2048]{1,0:T(8,128)(2,1)S(1)} fusion(bf16[256,2048]{1,0:T(8,128)(2,1)S(1)} %copy-done.5, bf16[128,384]{1,0:T(8,128)(2,1)} %bitcast.178), kind=kOutput, calls=%fused_computation.12 | convolution fusion | flops 134479872 | bytes 1638400 | tf_op jit(solution)/shard_map/dot_general | solution.py:492
  21.2 1.5 %convolution_convert_fusion.3 = bf16[64,2048]{1,0:T(8,128)(2,1)S(1)} fusion(bf16[64,256]{1,0:T(8,128)(2,1)S(1)} %convert.34, bf16[256,2048]{1,0:T(8,128)(2,1)} %param.50), kind=kOutput, calls=%fused_computation.14 | convolution fusion | flops 67239936 | bytes 1343488 | tf_op jit(solution)/shard_map/dot_general | solution.py:488
  22.8 1.0 fusion.25
  24.0 1.3 %fusion.16 = f32[128,768]{1,0:T(8,128)} fusion(f32[128,768]{1,0:T(8,128)S(1)} %fusion.119, bf16[256,192]{0,1:T(8,128)(2,1)S(1)} %copy-done.17, s32[768]{0:T(1024)S(1)} %copy-done.24, bf16[128,384]{1,0:T(8,128)(2,1)S(1)} %bitcast.180), kind=kOutput, calls=%fused_computation.41 | convolution fusion | flops 126271488 | bytes 954368 | tf_op jit(solution)/shard_map/dot_general | solution.py:89
  25.3 1.2 %convolution_add_fusion.7 = f32[128,256]{1,0:T(8,128)S(1)} fusion(f32[128,768]{1,0:T(8,128)} %fusion.16, bf16[128,384]{1,0:T(8,128)(2,1)S(1)} %bitcast.181, s32[256]{0:T(256)S(1)} %copy-done.25), kind=kOutput, calls=%fused_computation.68 | convolution fusion | flops 295680 | bytes 558080 | tf_op jit(solution)/shard_map/dot_general | solution.py:73
  27.8 2.1 %fusion.27 = f32[64,768]{1,0:T(8,128)} fusion(f32[768,64]{0,1:T(8,128)S(1)} %fusion.120, bf16[64,256]{1,0:T(8,128)(2,1)S(1)} %convert.34, bf16[256,192]{0,1:T(8,128)(2,1)} %param.53, s32[768]{0:T(1024)S(1)} %copy-done.24), kind=kOutput, calls=%fused_computation.56 | convolution fusion | flops 101056512 | bytes 527360 | tf_op jit(solution)/shard_map/dot_general | solution.py:89
  29.9 1.1 %fusion.30 = f32[64,256]{1,0:T(8,128)S(1)} fusion(f32[64,768]{1,0:T(8,128)} %fusion.27, s32[256]{0:T(256)S(1)} %copy-done.25, f32[12,64]{1,0:T(8,128)S(1)} %copy-done.15), kind=kOutput, calls=%fused_computation.70 | convolution fusion | flops 639744 | bytes 265216 | tf_op jit(solution)/shard_map/dot_general | solution.py:73
  31.2 1.6 %fusion.169 = (f32[8,64]{1,0:T(8,128)S(1)}, f32[8,64,128]{2,1,0:T(8,128)S(1)}) fusion(f32[8,64,128]{2,1,0:T(8,128)} %fusion.25, f32[128,256]{1,0:T(8,128)S(1)} %convolution_add_fusion.7, f32[8,256]{1,0:T(8,128)S(1)} %fusion.142, f32[64,256]{1,0:T(8,128)S(1)} %fusion.30, f32[8,128]{1,0:T(8,128)S(1)} %fusion.101, f32[8,64]{1,0:T(8,128)S(1)} %fusion.116, ...), kind=kOutput, calls=%fused_computation.280 | convolution fusion | flops 201981440 | bytes 737440 | tf_op jit(solution)/shard_map/dot_general | solution.py:115
  35.5 1.0 fusion.12
  38.6 12.7 %shard_map.428 = (bf16[4,16,3456]{2,1,0:T(8,128)(2,1)}, f32[4,16,128]{2,1,0:T(8,128)}) custom-call(bf16[4,16,3456]{2,1,0:T(8,128)(2,1)} %bitcast.186, f32[4,16,128]{2,1,0:T(8,128)} %bitcast.202), custom_call_target="tpu_custom_call" | custom-call | tf_op jit(solution)/shard_map/pallas_call | solution.py:316
  52.1 0.9 multiply_reduce_fusion.4
  54.5 1.1 %fusion.36 = f32[16,3360]{1,0:T(8,128)S(1)} fusion(f32[4,16,288]{2,1,0:T(8,128)S(1)} %reshape.282, f32[4,16,1024]{2,1,0:T(8,128)S(1)} %reshape.281, f32[4,16,2048]{2,1,0:T(8,128)S(1)} %reshape.280, bf16[4,16,3456]{2,1,0:T(8,128)(2,1)} %get-tuple-element.5), kind=kLoop, calls=%fused_computation.81 | loop fusion | flops 1021440 | bytes 1505280 | tf_op jit(solution)/shard_map/reduce_sum | solution.py:555
  59.4 12.8 %shard_map.429 = bf16[4,8,16,256]{3,2,1,0:T(8,128)(2,1)} custom-call(bf16[16,256]{1,0:T(8,128)(2,1)} %multiply_convert_fusion.x_ref), custom_call_target="tpu_custom_call" | custom-call | tf_op jit(solution)/shard_map/pallas_call | solution.py:371
  72.2 1.0 copy.94
  73.9 3.8 %fusion.171 = (f32[4,512]{1,0:T(4,128)S(1)}, f32[4,512,512]{1,2,0:T(8,128)}) fusion(pred[512]{0:T(512)(128)(4,1)S(1)} %broadcast_compare_fusion, bf16[512,4,64]{0,2,1:T(8,128)(2,1)S(1)} %bitcast.192, bf16[512,4,64]{0,2,1:T(8,128)(2,1)S(1)} %bitcast.195), kind=kOutput, calls=%fused_computation.282 | convolution fusion | flops 139461120 | bytes 4727296 | tf_op jit(solution)/shard_map/sub | solution.py:153
  77.7 2.7 %fusion.18 = bf16[4,64,512]{2,1,0:T(8,128)(2,1)S(1)} fusion(bf16[512,4,64]{0,2,1:T(8,128)(2,1)S(1)} %bitcast.193, f32[4,512,512]{1,2,0:T(8,128)} %get-tuple-element.41, f32[4,512]{1,0:T(4,128)S(1)} %get-tuple-element.40), kind=kOutput, calls=%fused_computation.45 | convolution fusion | flops 136445952 | bytes 4726784 | tf_op jit(solution)/shard_map/hij,jhd->ihd/dot_general | solution.py:155
  81.1 1.5 %fusion.173 = (f32[512]{0:T(512)S(1)}, f32[512,256]{1,0:T(8,128)S(1)}) fusion(bf16[2,256,256]{2,1,0:T(8,128)(2,1)} %param.64, f32[512,256]{1,0:T(8,128)S(1)} %get-tuple-element.43, f32[256]{0:T(256)S(1)} %bitcast.210, f32[512]{0:T(512)S(1)} %add_rsqrt_fusion.1, f32[512]{0:T(512)S(1)} %broadcast_multiply_fusion.1, bf16[2,256,256]{2,1,0:T(8,128)(2,1)} %param.63), kind=kOutput, calls=%fused_computation.284 | convolution fusion | flops 135659008 | bytes 1847296 | tf_op jit(solution)/shard_map/dot_general | solution.py:166
  83.8 1.9 %fusion.178 = (f32[4,192]{1,0:T(4,128)S(1)}, f32[4,192,512]{2,1,0:T(8,128)}) fusion(bf16[192,4,64]{0,2,1:T(8,128)(2,1)S(1)} %bitcast.199, bf16[512,4,64]{0,2,1:T(8,128)(2,1)S(1)} %bitcast.196, pred[512]{0:T(512)(128)(4,1)S(1)} %broadcast_compare_fusion), kind=kOutput, calls=%fused_computation.285 | convolution fusion | flops 52298240 | bytes 1936896 | tf_op jit(solution)/shard_map/sub | solution.py:153
  85.7 1.9 %convolution_convert_fusion.10 = bf16[4,64,192]{2,1,0:T(8,128)(2,1)S(1)} fusion(bf16[512,4,64]{0,2,1:T(8,128)(2,1)S(1)} %bitcast.194, f32[4,192,512]{2,1,0:T(8,128)} %get-tuple-element.47, f32[4,192]{1,0:T(4,128)S(1)} %get-tuple-element.46), kind=kOutput, calls=%fused_computation.61 | convolution fusion | flops 51167232 | bytes 1936384 | tf_op jit(solution)/shard_map/hij,jhd->ihd/dot_general | solution.py:155
  92.8 12.3 %shard_map.430 = bf16[64,128,128]{2,1,0:T(8,128)(2,1)} custom-call(bf16[64,128,128]{2,1,0:T(8,128)(2,1)} %copy-done.1, f32[64,384]{1,0:T(8,128)} %fusion.71.row_ref, f32[128,384]{1,0:T(8,128)} %convolution_add_fusion.3.key_ref, f32[64,128]{1,0:T(8,128)} %broadcast_in_dim.79.live_row, f32[128,128]{1,0:T(8,128)} %broadcast_in_dim.80.live_key, ...), custom_call_target="tpu_custom_call" | custom-call | tf_op jit(solution)/shard_map/pallas_call | solution.py:414
  (184 shorter events, 27.5 us)
Async XLA Ops:
  0.6 57.4 %copy-start = (bf16[3456,256]{1,0:T(8,128)(2,1)S(1)}, bf16[3456,256]{1,0:T(8,128)(2,1)}, u32[]{:S(2)}) copy-start(bf16[3456,256]{1,0:T(8,128)(2,1)} %param.59) | copy-start | bytes 5308420
  4.0 2.2 %copy-start.10 = (f32[128,128]{1,0:T(8,128)S(1)}, f32[128,128]{1,0:T(8,128)}, u32[]{:S(2)}) copy-start(f32[128,128]{1,0:T(8,128)} %param.58) | copy-start | bytes 196612
  7.7 2.2 %copy-start.30 = (bf16[128,8]{0,1:T(8,128)(2,1)S(1)}, bf16[128,8]{0,1:T(8,128)(2,1)}, u32[]{:S(2)}) copy-start(bf16[128,8]{0,1:T(8,128)(2,1)} %param.56) | copy-start | bytes 6148
  9.9 10.0 %copy-start.5 = (bf16[256,2048]{1,0:T(8,128)(2,1)S(1)}, bf16[256,2048]{1,0:T(8,128)(2,1)}, u32[]{:S(2)}) copy-start(bf16[256,2048]{1,0:T(8,128)(2,1)} %param.51) | copy-start | bytes 3145732
  19.9 3.9 %copy-start.4 = (bf16[2,64,384]{2,1,0:T(8,128)(2,1)S(1)}, bf16[2,64,384]{2,1,0:T(8,128)(2,1)}, u32[]{:S(2)}) copy-start(bf16[2,64,384]{2,1,0:T(8,128)(2,1)} %shard_map.427) | copy-start | bytes 294916
  20.0 3.8 %copy-start.18 = (s32[768]{0:T(1024)S(1)}, s32[768]{0:T(1024)}, u32[]{:S(2)}) copy-start(s32[768]{0:T(1024)} %constant.100.clone) | copy-start | bytes 9220
  20.0 4.0 %copy-start.17 = (bf16[256,192]{0,1:T(8,128)(2,1)S(1)}, bf16[256,192]{0,1:T(8,128)(2,1)}, u32[]{:S(2)}) copy-start(bf16[256,192]{0,1:T(8,128)(2,1)} %param.54) | copy-start | bytes 294916
  20.0 4.0 %copy-start.24 = (s32[768]{0:T(1024)S(1)}, s32[768]{0:T(1024)}, u32[]{:S(2)}) copy-start(s32[768]{0:T(1024)} %constant.99.clone) | copy-start | bytes 9220
  21.2 4.1 %copy-start.25 = (s32[256]{0:T(256)S(1)}, s32[256]{0:T(256)}, u32[]{:S(2)}) copy-start(s32[256]{0:T(256)} %constant.101.clone) | copy-start | bytes 3076
  21.2 5.3 %copy-start.19 = (s32[256]{0:T(256)S(1)}, s32[256]{0:T(256)}, u32[]{:S(2)}) copy-start(s32[256]{0:T(256)} %constant.105.clone) | copy-start | bytes 3076
  22.8 8.4 %copy-start.35 = (f32[8]{0:T(128)S(1)}, f32[8]{0:T(128)}, u32[]{:S(2)}) copy-start(f32[8]{0:T(128)} %param.57) | copy-start | bytes 100
  23.8 10.0 %copy-start.6 = (bf16[256,2048]{1,0:T(8,128)(2,1)S(1)}, bf16[256,2048]{1,0:T(8,128)(2,1)}, u32[]{:S(2)}) copy-start(bf16[256,2048]{1,0:T(8,128)(2,1)} %param.52) | copy-start | bytes 3145732
  34.4 2.1 %copy-start.20 = (s32[1152]{0:T(1024)S(1)}, s32[1152]{0:T(1024)}, u32[]{:S(2)}) copy-start(s32[1152]{0:T(1024)} %constant.103.clone) | copy-start | bytes 13828
  53.9 2.7 %copy-start.23 = (s32[1152]{0:T(1024)S(1)}, s32[1152]{0:T(1024)}, u32[]{:S(2)}) copy-start(s32[1152]{0:T(1024)} %constant.107.clone) | copy-start | bytes 13828
  54.5 4.2 %copy-start.31 = (f32[256]{0:T(256)S(1)}, f32[256]{0:T(256)}, u32[]{:S(2)}) copy-start(f32[256]{0:T(256)} %param.60) | copy-start | bytes 3076
  55.6 17.5 %copy-start.7 = (bf16[2,256,768]{2,1,0:T(8,128)(2,1)S(1)}, bf16[2,256,768]{2,1,0:T(8,128)(2,1)}, u32[]{:S(2)}) copy-start(bf16[2,256,768]{2,1,0:T(8,128)(2,1)} %param.61) | copy-start | bytes 2359300
  77.7 2.7 %copy-start.11 = (bf16[2,256,256]{2,1,0:T(8,128)(2,1)S(1)}, bf16[2,256,256]{2,1,0:T(8,128)(2,1)}, u32[]{:S(2)}) copy-start(bf16[2,256,256]{2,1,0:T(8,128)(2,1)} %param.62) | copy-start | bytes 786436
  77.7 3.4 %copy-start.26 = (f32[2,2,256]{2,1,0:T(2,128)S(1)}, f32[2,2,256]{2,1,0:T(2,128)}, u32[]{:S(2)}) copy-start(f32[2,2,256]{2,1,0:T(2,128)} %param.65) | copy-start | bytes 12292
  85.7 2.0 %copy-start.12 = (bf16[2,256,256]{2,1,0:T(8,128)(2,1)S(1)}, bf16[2,256,256]{2,1,0:T(8,128)(2,1)}, u32[]{:S(2)}) copy-start(bf16[2,256,256]{2,1,0:T(8,128)(2,1)} %param.62) | copy-start | bytes 786436
  85.7 2.5 %copy-start.32 = (bf16[2,256,256]{2,1,0:T(8,128)(2,1)S(1)}, bf16[2,256,256]{2,1,0:T(8,128)(2,1)}, u32[]{:S(2)}) copy-start(bf16[2,256,256]{2,1,0:T(8,128)(2,1)} %param.64) | copy-start | bytes 786436
  85.7 2.5 %copy-start.33 = (bf16[2,256,256]{2,1,0:T(8,128)(2,1)S(1)}, bf16[2,256,256]{2,1,0:T(8,128)(2,1)}, u32[]{:S(2)}) copy-start(bf16[2,256,256]{2,1,0:T(8,128)(2,1)} %param.63) | copy-start | bytes 786436
  87.7 2.0 %copy-start.9 = (bf16[256,768]{1,0:T(8,128)(2,1)S(1)}, bf16[256,768]{1,0:T(8,128)(2,1)}, u32[]{:S(2)}) copy-start(bf16[256,768]{1,0:T(8,128)(2,1)} %param.67) | copy-start | bytes 1179652
  90.5 14.7 %copy-start.8 = (f32[64,256]{1,0:T(8,128)}, f32[64,256]{1,0:T(8,128)S(1)}, u32[]{:S(2)}) copy-start(f32[64,256]{1,0:T(8,128)S(1)} %slice.265) | copy-start | bytes 196612
  92.8 12.4 %copy-start.22 = (f32[256,6]{0,1:T(8,128)S(1)}, f32[256,6]{0,1:T(8,128)}, u32[]{:S(2)}) copy-start(f32[256,6]{0,1:T(8,128)} %param.66) | copy-start | bytes 18436
  (13 other events, 17.3 us)

commit v2 on v1

--- a/solution.py
+++ b/solution.py
@@ -141,30 +141,128 @@
     )
 
 
-def encoder_core(states, query_half, key_value, valid, output, expand, shrink, scales):
-    queries = head_split(query_half, TF_HD)
-    key_vectors = head_split(key_value[:, :C_S], TF_HD)
-    value_vectors = head_split(key_value[:, C_S:], TF_HD)
-    scores = jnp.einsum(
-        "ihd,jhd->hij", queries, key_vectors, preferred_element_type=jnp.float32
-    ) / math.sqrt(TF_HD)
-    masked = jnp.where(valid[None, None, :], scores, NEG_FILL)
-    row_top = jnp.max(masked, axis=-1, keepdims=True)
-    weights = jnp.where(valid[None, None, :], jnp.exp(masked - row_top), 0.0)
-    attention = (weights / jnp.sum(weights, axis=-1, keepdims=True)).astype(jnp.bfloat16)
-    context = jnp.einsum(
-        "hij,jhd->ihd", attention, value_vectors, preferred_element_type=jnp.float32
-    ).astype(jnp.bfloat16)
-    context = context.reshape(states.shape[0], C_S)
+def encoder_rows(states, key_value, fill, project, output, expand, shrink, scales):
+    queries = jnp.dot(
+        states.astype(jnp.bfloat16), project[:, :C_S], preferred_element_type=jnp.float32
+    ).astype(jnp.bfloat16) * jnp.asarray(1.0 / math.sqrt(TF_HD), jnp.bfloat16)
+    owner = lax.broadcasted_iota(jnp.int32, (1, C_S), 1) // TF_HD
+    context = jnp.zeros(states.shape, jnp.float32)
+    for head in range(C_S // TF_HD):
+        mine = owner == head
+        only = jnp.where(mine, 1.0, 0.0)
+        scores = lax.dot_general(
+            queries * only.astype(jnp.bfloat16),
+            key_value[:, :C_S],
+            (((1,), (1,)), ((), ())),
+            preferred_element_type=jnp.float32,
+        )
+        scores = scores + fill
+        weights = jnp.exp(scores - jnp.max(scores, axis=-1, keepdims=True))
+        inverse = 1.0 / jnp.sum(weights, axis=-1, keepdims=True)
+        mixed = jnp.dot(
+            weights.astype(jnp.bfloat16),
+            key_value[:, C_S:],
+            preferred_element_type=jnp.float32,
+        )
+        context = context + mixed * (inverse * only)
     middle = layer_norm(
-        states + jnp.dot(context, output, preferred_element_type=jnp.float32), scales[0]
-    )
-    hidden = jax.nn.relu(
-        jnp.dot(middle.astype(jnp.bfloat16), expand, preferred_element_type=jnp.float32)
+        states
+        + jnp.dot(context.astype(jnp.bfloat16), output, preferred_element_type=jnp.float32),
+        scales[0:1],
+    )
+    hidden = jnp.maximum(
+        jnp.dot(middle.astype(jnp.bfloat16), expand, preferred_element_type=jnp.float32), 0.0
     ).astype(jnp.bfloat16)
     return layer_norm(
-        middle + jnp.dot(hidden, shrink, preferred_element_type=jnp.float32), scales[1]
-    )
+        middle + jnp.dot(hidden, shrink, preferred_element_type=jnp.float32), scales[1:2]
+    )
+
+
+def encoder_kernel(
+    states_ref,
+    fill_ref,
+    project,
+    output,
+    expand,
+    shrink,
+    scales,
+    to_edge,
+    bias,
+    second_ref,
+    row_ref,
+    key_ref,
+    old,
+    new,
+    key_value,
+):
+    count = states_ref.shape[0]
+    rows, keys = row_ref.shape[0], key_ref.shape[0]
+    chunk = math.gcd(count, 128)
+
+    def apply(states, layer):
+        return encoder_rows(
+            states,
+            key_value[...],
+            fill_ref[...],
+            project[layer],
+            output[layer],
+            expand[layer],
+            shrink[layer],
+            scales[layer],
+        )
+
+    old[...] = states_ref[...].astype(jnp.float32)
+    buffers = (old, new)
+    for layer in range(LAYERS):
+        source, target = buffers[layer % 2], buffers[(layer + 1) % 2]
+        key_value[...] = jnp.dot(
+            source[...].astype(jnp.bfloat16),
+            project[layer][:, C_S:],
+            preferred_element_type=jnp.float32,
+        ).astype(jnp.bfloat16)
+        if layer < LAYERS - 1:
+
+            def step(index, carry):
+                window = pl.ds(pl.multiple_of(index * chunk, chunk), chunk)
+                target[window, :] = apply(source[window, :], layer)
+                return carry
+
+            lax.fori_loop(0, count // chunk, step, 0)
+        else:
+            row_first = pl.multiple_of(lax.axis_index("pb") * rows, rows)
+            key_first = pl.multiple_of(lax.axis_index("ka") * keys, keys)
+            second = apply(source[pl.ds(row_first, rows), :], layer)
+            second_ref[...] = second
+            row_ref[...] = jnp.dot(
+                second.astype(jnp.bfloat16), to_edge[:, :EH], preferred_element_type=jnp.float32
+            )
+            final = apply(source[pl.ds(key_first, keys), :], layer)
+            key_ref[...] = (
+                jnp.dot(
+                    final.astype(jnp.bfloat16), to_edge[:, EH:], preferred_element_type=jnp.float32
+                )
+                + bias[...]
+            )
+
+
+def encode(states, valid, rows, keys, project, output, expand, shrink, scales, to_edge, bias):
+    fill = jnp.where(valid, 0.0, NEG_FILL)[None]
+    count = states.shape[0]
+    return pl.pallas_call(
+        encoder_kernel,
+        out_shape=(
+            jax.ShapeDtypeStruct((rows, C_S), jnp.float32),
+            jax.ShapeDtypeStruct((rows, EH), jnp.float32),
+            jax.ShapeDtypeStruct((keys, EH), jnp.float32),
+        ),
+        in_specs=[pl.BlockSpec(memory_space=pltpu.VMEM)] * 9,
+        out_specs=(pl.BlockSpec(memory_space=pltpu.VMEM),) * 3,
+        scratch_shapes=[
+            pltpu.VMEM((count, C_S), jnp.float32),
+            pltpu.VMEM((count, C_S), jnp.float32),
+            pltpu.VMEM((count, 2 * C_S), jnp.bfloat16),
+        ],
+    )(states, fill, project, output, expand, shrink, scales, to_edge, bias[None])
 
 
 def update_frames(states, frames, frame_weight):
@@ -563,52 +661,25 @@
         attention_scales,
     )
     every_valid = padding_mask == 1
-    whole_states = gather_rows(first_states.astype(jnp.bfloat16), n_pb, n_ka).astype(
-        first_states.dtype
-    )
-    for layer_number in range(LAYERS):
-        projection = layer_project[layer_number]
-        key_value = jnp.dot(
-            whole_states.astype(jnp.bfloat16),
-            projection[:, C_S:],
-            preferred_element_type=jnp.float32,
-        ).astype(jnp.bfloat16)
-        if layer_number == LAYERS - 1:
-            whole_states = jnp.concatenate(
-                [
-                    lax.dynamic_slice_in_dim(whole_states, row_first, row_count, 0),
-                    lax.dynamic_slice_in_dim(whole_states, key_first, key_count, 0),
-                ],
-                axis=0,
-            )
-        query_half = jnp.dot(
-            whole_states.astype(jnp.bfloat16),
-            projection[:, :C_S],
-            preferred_element_type=jnp.float32,
-        ).astype(jnp.bfloat16)
-        whole_states = encoder_core(
-            whole_states,
-            query_half,
-            key_value,
-            every_valid,
-            layer_output[layer_number],
-            layer_expand[layer_number],
-            layer_shrink[layer_number],
-            layer_scales[layer_number],
-        )
-    second_states = whole_states[:row_count]
-    key_second = whole_states[row_count:]
+    whole_states = gather_rows(first_states.astype(jnp.bfloat16), n_pb, n_ka)
+    second_states, row_project, key_project = encode(
+        whole_states,
+        every_valid,
+        row_count,
+        key_count,
+        layer_project,
+        layer_output,
+        layer_expand,
+        layer_shrink,
+        layer_scales,
+        node_to_edge,
+        edge_biases[0],
+    )
     frames_out = update_frames(second_states, frames, frame_weight)
-    row_project = jnp.dot(
-        second_states.astype(jnp.bfloat16), node_to_edge[:, :EH], preferred_element_type=jnp.float32
-    )
-    key_project = jnp.dot(
-        key_second.astype(jnp.bfloat16), node_to_edge[:, EH:], preferred_element_type=jnp.float32
-    )
     edges_out = edge_transition(
         pair_rep,
         row_project,
-        key_project + edge_biases[0],
+        key_project,
         mask_rows,
         mask_keys,
         (edge_first, edge_second, edge_third),

time: 108 us -> 107 us (level)
  Pallas kernels: 46.3 us -> 62.3 us
  matrix products: 38.4 us -> 23.9 us
  other arithmetic: 10 us -> 7.67 us
    pallas_call x0 -> x1, Pallas kernels: none -> 16 us  [encode(): pl.pallas_call(encoder_kernel, out_shape=(jax.ShapeDtypeStruct((rows, C_S...]
    dot_general x12 -> x0, matrix products: 10.1 us -> none  [the longest x2 4.65 us: encoder_core(): jnp.einsum('hij,jhd->ihd', attention, value_vectors, preferred_element_ty...]
    sub x2 -> x0, matrix products: 5.69 us -> none  [encoder_core(): weights = jnp.where(valid[None, None, :], jnp.exp(masked - row_top), 0.0)]
    dot_general x3, matrix products: 4.36 us -> 6.27 us  [place_points(): local = jnp.dot(features, spread, preferred_element_type=jnp.float32)]
    unnamed x76 -> x58, local copies, waits for them, and re-layouts: 2.48 us -> 2.47 us
where the time goes in v2:
time: 107 us; the launch traced here: 106 us
  Pallas kernels  62.3 us (58%)
  matrix products  23.9 us (22%)
  local copies, waits for them, and re-layouts  11.2 us (10%)
  other arithmetic  7.67 us (7%)
  between operations  1.33 us (1%)
    pallas_call x1, Pallas kernels, encode(): pl.pallas_call(encoder_kernel, out_shape=(jax.ShapeDtypeStruct((rows, C_S...  16 us
    pallas_call x1, Pallas kernels, gather_rows(): pl.pallas_call(functools.partial(gather_kernel, n_pb, n_ka), out_shape=ja...  12.8 us
    pallas_call x1, Pallas kernels, exchange(): pl.pallas_call(functools.partial(exchange_kernel, n_ka), out_shape=(jax.S...  12.7 us
    pallas_call x1, Pallas kernels, edge_transition(): pl.pallas_call(edge_kernel, grid=(rows // step,), out_shape=jax.ShapeDtyp...  12.4 us
    pallas_call x1, Pallas kernels, key_tile(): pl.pallas_call(functools.partial(key_tile_kernel, n_pb, n_ka), out_shape=...  8.41 us
    dot_general x3, matrix products, place_points(): local = jnp.dot(features, spread, preferred_element_type=jnp.float32)  6.27 us
    dot_general x4, matrix products, offset_lanes(): jnp.dot(offset, pick(np.where(real, comp, -1), 3, jnp.float32), precision...  2.87 us
    unnamed x58, local copies, waits for them, and re-layouts  2.47 us

profile of v2, /device:TPU:1, one launch (start us, length us, event | category | flops | bytes accessed | tf_op | source)
XLA Modules:
  0.0 106.4 jit_solution(1073070570438434381)
XLA Ops:
  0.7 0.9 dynamic_slice.26
  4.0 2.2 %fusion = f32[8192,128]{1,0:T(8,128)S(1)} fusion(s32[8192]{0:T(1024)S(1)} %fusion.71, f32[128,128]{1,0:T(8,128)} %param.58), kind=kOutput, calls=%fused_computation.3 | convolution fusion | flops 269516800 | bytes 4292608 | tf_op jit(solution)/shard_map/dot_general | solution.py:606
  6.2 1.3 %convolution_add_fusion = f32[8192,128]{1,0:T(8,128)S(1)} fusion(f32[8192,128]{1,0:T(8,128)S(1)} %fusion, s32[8192]{0:T(1024)S(1)} %fusion.71, f32[128,128]{1,0:T(8,128)S(1)} %copy-done.8), kind=kOutput, calls=%fused_computation | convolution fusion | flops 270581760 | bytes 8486912 | tf_op jit(solution)/shard_map/dot_general | solution.py:607
  7.7 0.8 add_convert_fusion.pair_ref
  8.6 1.3 %copy-done.1 = bf16[64,128,128]{2,1,0:T(8,128)(2,1)} copy-done((bf16[64,128,128]{2,1,0:T(8,128)(2,1)}, bf16[64,128,128]{2,1,0:T(8,128)(2,1)S(1)}, u32[]{:S(2)}) %copy-start.1) | copy-done | bytes 2097176
  11.5 8.4 %shard_map.427 = bf16[2,64,384]{2,1,0:T(8,128)(2,1)} custom-call(bf16[64,384]{1,0:T(8,128)(2,1)} %fusion.59.x_ref), custom_call_target="tpu_custom_call" | custom-call | tf_op jit(solution)/shard_map/pallas_call | solution.py:374
  20.0 1.2 %convolution_convert_fusion.1 = bf16[128,2048]{1,0:T(8,128)(2,1)S(1)} fusion(bf16[256,2048]{1,0:T(8,128)(2,1)S(1)} %copy-done.5, bf16[128,384]{1,0:T(8,128)(2,1)} %bitcast.112), kind=kOutput, calls=%fused_computation.6 | convolution fusion | flops 134479872 | bytes 1638400 | tf_op jit(solution)/shard_map/dot_general | solution.py:590
  21.2 1.5 %convolution_convert_fusion.3 = bf16[64,2048]{1,0:T(8,128)(2,1)S(1)} fusion(bf16[64,256]{1,0:T(8,128)(2,1)S(1)} %convert.31, bf16[256,2048]{1,0:T(8,128)(2,1)} %param.50), kind=kOutput, calls=%fused_computation.8 | convolution fusion | flops 67239936 | bytes 1343488 | tf_op jit(solution)/shard_map/dot_general | solution.py:586
  22.8 1.0 fusion.15
  24.0 2.3 %fusion.8 = f32[128,768]{1,0:T(8,128)} fusion(f32[128,768]{1,0:T(8,128)S(1)} %fusion.60, bf16[256,192]{0,1:T(8,128)(2,1)} %param.54, s32[768]{0:T(1024)S(1)} %copy-done.18, bf16[128,384]{1,0:T(8,128)(2,1)S(1)} %bitcast.114), kind=kOutput, calls=%fused_computation.22 | convolution fusion | flops 126271488 | bytes 954368 | tf_op jit(solution)/shard_map/dot_general | solution.py:89
  26.3 1.2 %convolution_add_fusion.2 = f32[128,256]{1,0:T(8,128)S(1)} fusion(f32[128,768]{1,0:T(8,128)} %fusion.8, bf16[128,384]{1,0:T(8,128)(2,1)S(1)} %bitcast.115, s32[256]{0:T(256)S(1)} %copy-done.19), kind=kOutput, calls=%fused_computation.39 | convolution fusion | flops 295680 | bytes 558080 | tf_op jit(solution)/shard_map/dot_general | solution.py:73
  28.1 2.1 %fusion.17 = f32[64,768]{1,0:T(8,128)} fusion(f32[768,64]{0,1:T(8,128)S(1)} %fusion.61, bf16[64,256]{1,0:T(8,128)(2,1)S(1)} %convert.31, bf16[256,192]{0,1:T(8,128)(2,1)} %param.53, s32[768]{0:T(1024)S(1)} %copy-done.18), kind=kOutput, calls=%fused_computation.34 | convolution fusion | flops 101056512 | bytes 527360 | tf_op jit(solution)/shard_map/dot_general | solution.py:89
  30.2 1.1 %fusion.19 = f32[64,256]{1,0:T(8,128)S(1)} fusion(f32[64,768]{1,0:T(8,128)} %fusion.17, s32[256]{0:T(256)S(1)} %copy-done.19, f32[12,64]{1,0:T(8,128)S(1)} %copy-done.9), kind=kOutput, calls=%fused_computation.41 | convolution fusion | flops 639744 | bytes 265216 | tf_op jit(solution)/shard_map/dot_general | solution.py:73
  31.5 1.6 %fusion.98 = (f32[8,64]{1,0:T(8,128)S(1)}, f32[8,64,128]{2,1,0:T(8,128)S(1)}) fusion(f32[8,64,128]{2,1,0:T(8,128)} %fusion.15, f32[128,256]{1,0:T(8,128)S(1)} %convolution_add_fusion.2, f32[8,256]{1,0:T(8,128)S(1)} %fusion.82, f32[64,256]{1,0:T(8,128)S(1)} %fusion.19, f32[8,128]{1,0:T(8,128)S(1)} %fusion.50, f32[8,64]{1,0:T(8,128)S(1)} %fusion.57, ...), kind=kOutput, calls=%fused_computation.184 | convolution fusion | flops 201981440 | bytes 737440 | tf_op jit(solution)/shard_map/dot_general | solution.py:115
  35.8 1.9 %fusion.4 = f32[128,1152]{1,0:T(8,128)S(1)} fusion(bf16[256,288]{0,1:T(8,128)(2,1)} %param.55, s32[1152]{0:T(1024)S(1)} %copy-done.26, bf16[128,384]{1,0:T(8,128)(2,1)S(1)} %bitcast.117), kind=kOutput, calls=%fused_computation.16 | convolution fusion | flops 245993472 | bytes 811008 | tf_op jit(solution)/shard_map/dot_general | solution.py:89
  38.1 0.8 fusion.5
  39.0 0.8 fusion.35
  39.8 12.7 %shard_map.428 = (bf16[4,16,3456]{2,1,0:T(8,128)(2,1)}, f32[4,16,128]{2,1,0:T(8,128)}) custom-call(bf16[4,16,3456]{2,1,0:T(8,128)(2,1)} %bitcast.120, f32[4,16,128]{2,1,0:T(8,128)} %bitcast.129), custom_call_target="tpu_custom_call" | custom-call | tf_op jit(solution)/shard_map/pallas_call | solution.py:414
  52.5 0.8 slice_reduce_fusion
  53.4 0.9 multiply_reduce_fusion
  58.9 12.8 %shard_map.429 = bf16[4,8,16,256]{3,2,1,0:T(8,128)(2,1)} custom-call(bf16[16,256]{1,0:T(8,128)(2,1)} %multiply_convert_fusion.x_ref), custom_call_target="tpu_custom_call" | custom-call | tf_op jit(solution)/shard_map/pallas_call | solution.py:469
  71.7 1.7 %copy.89 = bf16[8,4,16,256]{3,2,1,0:T(8,128)(2,1)} copy(bf16[8,4,16,256]{3,2,0,1:T(8,128)(2,1)} %bitcast.123) | data formatting | bytes 524288 | tf_op jit(solution)/shard_map/transpose | solution.py:481
  74.6 16.0 %shard_map.430 = (f32[64,256]{1,0:T(8,128)}, f32[64,384]{1,0:T(8,128)}, f32[128,384]{1,0:T(8,128)}) custom-call(bf16[512,256]{1,0:T(8,128)(2,1)} %bitcast.124, f32[1,512]{1,0:T(1,128)} %bitcast.134, bf16[2,256,768]{2,1,0:T(8,128)(2,1)} %project.1, bf16[2,256,256]{2,1,0:T(8,128)(2,1)} %output.1, bf16[2,256,256]{2,1,0:T(8,128)(2,1)} %expand.1, ...), custom_call_target="tpu_custom_call" | custom-call | tf_op jit(solution)/shard_map/pallas_call | solution.py:251
  92.1 12.4 %shard_map.431 = bf16[64,128,128]{2,1,0:T(8,128)(2,1)} custom-call(bf16[64,128,128]{2,1,0:T(8,128)(2,1)} %copy-done.1, f32[64,384]{1,0:T(8,128)} %get-tuple-element.11.row_ref, f32[128,384]{1,0:T(8,128)} %get-tuple-element.12.key_ref, f32[64,128]{1,0:T(8,128)} %broadcast_in_dim.52.live_row, f32[128,128]{1,0:T(8,128)} %broadcast_in_dim.53.live_key, ...), custom_call_target="tpu_custom_call" | custom-call | tf_op jit(solution)/shard_map/pallas_call | solution.py:512
  (131 shorter events, 17.3 us)
Async XLA Ops:
  0.6 56.9 %copy-start = (bf16[3456,256]{1,0:T(8,128)(2,1)S(1)}, bf16[3456,256]{1,0:T(8,128)(2,1)}, u32[]{:S(2)}) copy-start(bf16[3456,256]{1,0:T(8,128)(2,1)} %param.59) | copy-start | bytes 5308420
  4.0 2.2 %copy-start.8 = (f32[128,128]{1,0:T(8,128)S(1)}, f32[128,128]{1,0:T(8,128)}, u32[]{:S(2)}) copy-start(f32[128,128]{1,0:T(8,128)} %param.58) | copy-start | bytes 196612
  6.1 1.6 %copy-start.3 = (bf16[64,128,128]{2,1,0:T(8,128)(2,1)S(1)}, bf16[64,128,128]{2,1,0:T(8,128)(2,1)}, u32[]{:S(2)}) copy-start(bf16[64,128,128]{2,1,0:T(8,128)(2,1)} %param.46) | copy-start | bytes 6291460
  7.7 2.2 %copy-start.23 = (bf16[128,8]{0,1:T(8,128)(2,1)S(1)}, bf16[128,8]{0,1:T(8,128)(2,1)}, u32[]{:S(2)}) copy-start(bf16[128,8]{0,1:T(8,128)(2,1)} %param.56) | copy-start | bytes 6148
  9.9 10.0 %copy-start.5 = (bf16[256,2048]{1,0:T(8,128)(2,1)S(1)}, bf16[256,2048]{1,0:T(8,128)(2,1)}, u32[]{:S(2)}) copy-start(bf16[256,2048]{1,0:T(8,128)(2,1)} %param.51) | copy-start | bytes 3145732
  19.9 3.8 %copy-start.4 = (bf16[2,64,384]{2,1,0:T(8,128)(2,1)S(1)}, bf16[2,64,384]{2,1,0:T(8,128)(2,1)}, u32[]{:S(2)}) copy-start(bf16[2,64,384]{2,1,0:T(8,128)(2,1)} %shard_map.427) | copy-start | bytes 294916
  19.9 3.8 %copy-start.12 = (s32[768]{0:T(1024)S(1)}, s32[768]{0:T(1024)}, u32[]{:S(2)}) copy-start(s32[768]{0:T(1024)} %constant.79.clone) | copy-start | bytes 9220
  20.0 4.0 %copy-start.18 = (s32[768]{0:T(1024)S(1)}, s32[768]{0:T(1024)}, u32[]{:S(2)}) copy-start(s32[768]{0:T(1024)} %constant.78.clone) | copy-start | bytes 9220
  21.2 5.1 %copy-start.19 = (s32[256]{0:T(256)S(1)}, s32[256]{0:T(256)}, u32[]{:S(2)}) copy-start(s32[256]{0:T(256)} %constant.80.clone) | copy-start | bytes 3076
  21.2 6.3 %copy-start.13 = (s32[256]{0:T(256)S(1)}, s32[256]{0:T(256)}, u32[]{:S(2)}) copy-start(s32[256]{0:T(256)} %constant.84.clone) | copy-start | bytes 3076
  21.2 6.5 %copy-start.22 = (s32[512]{0:T(512)S(1)}, s32[512]{0:T(512)}, u32[]{:S(2)}) copy-start(s32[512]{0:T(512)} %param.49) | copy-start | bytes 6148
  22.8 8.7 %copy-start.25 = (f32[8]{0:T(128)S(1)}, f32[8]{0:T(128)}, u32[]{:S(2)}) copy-start(f32[8]{0:T(128)} %param.57) | copy-start | bytes 100
  23.8 10.3 %copy-start.6 = (bf16[256,2048]{1,0:T(8,128)(2,1)S(1)}, bf16[256,2048]{1,0:T(8,128)(2,1)}, u32[]{:S(2)}) copy-start(bf16[256,2048]{1,0:T(8,128)(2,1)} %param.52) | copy-start | bytes 3145732
  33.5 1.6 %copy-start.2 = (bf16[64,128,128]{2,1,0:T(8,128)(2,1)S(1)}, bf16[64,128,128]{2,1,0:T(8,128)(2,1)}, u32[]{:S(2)}) copy-start(bf16[64,128,128]{2,1,0:T(8,128)(2,1)} %copy-done.1) | copy-start | bytes 6291460
  34.7 3.0 %copy-start.14 = (s32[1152]{0:T(1024)S(1)}, s32[1152]{0:T(1024)}, u32[]{:S(2)}) copy-start(s32[1152]{0:T(1024)} %constant.82.clone) | copy-start | bytes 13828
  35.1 2.8 %copy-start.15 = (s32[384]{0:T(512)S(1)}, s32[384]{0:T(512)}, u32[]{:S(2)}) copy-start(s32[384]{0:T(512)} %constant.83.clone) | copy-start | bytes 4612
  35.7 2.4 %copy-start.21 = (s32[384]{0:T(512)S(1)}, s32[384]{0:T(512)}, u32[]{:S(2)}) copy-start(s32[384]{0:T(512)} %constant.85.clone) | copy-start | bytes 4612
  52.5 3.2 %copy-start.7 = (bf16[4,16,3456]{2,1,0:T(8,128)(2,1)S(1)}, bf16[4,16,3456]{2,1,0:T(8,128)(2,1)}, u32[]{:S(2)}) copy-start(bf16[4,16,3456]{2,1,0:T(8,128)(2,1)} %get-tuple-element.8) | copy-start | bytes 1327108
  55.2 1.7 %copy-start.17 = (s32[1152]{0:T(1024)S(1)}, s32[1152]{0:T(1024)}, u32[]{:S(2)}) copy-start(s32[1152]{0:T(1024)} %constant.86.clone) | copy-start | bytes 13828
  55.3 1.9 %copy-start.27 = (s32[384]{0:T(512)S(1)}, s32[384]{0:T(512)}, u32[]{:S(2)}) copy-start(s32[384]{0:T(512)} %constant.87.clone) | copy-start | bytes 4612
  55.8 2.5 %copy-start.24 = (f32[256]{0:T(256)S(1)}, f32[256]{0:T(256)}, u32[]{:S(2)}) copy-start(f32[256]{0:T(256)} %param.60) | copy-start | bytes 3076
  55.9 17.5 %copy-start.20 = (f32[2,384]{1,0:T(2,128)S(1)}, f32[2,384]{1,0:T(2,128)}, u32[]{:S(2)}) copy-start(f32[2,384]{1,0:T(2,128)} %param.71) | copy-start | bytes 9220
  92.1 12.4 %copy-start.11 = (f32[64,256]{1,0:T(8,128)S(1)}, f32[64,256]{1,0:T(8,128)}, u32[]{:S(2)}) copy-start(f32[64,256]{1,0:T(8,128)} %get-tuple-element.5) | copy-start | bytes 196612
  92.1 12.4 %copy-start.16 = (f32[256,6]{0,1:T(8,128)S(1)}, f32[256,6]{0,1:T(8,128)}, u32[]{:S(2)}) copy-start(f32[256,6]{0,1:T(8,128)} %param.66) | copy-start | bytes 18436
  (4 other events, 4.4 us)
